TPU v7x, 256 devices: a whole 4x4x8 slice. The times are simulated.
256 devices in a mesh: ctx: 32 (over x, z), dp: 2 (over core), tp: 4 (over y).
Axes of the slice: x: 4, y: 4, z: 8, core: 2. Of those that a mesh axis runs over, the one named last changes fastest.
Arguments:
- ssm_input: bfloat16 [2, 4096, 8192], P('dp', 'ctx', 'tp'), may hold values from -12 to 12
- ssm_gate: bfloat16 [2, 4096, 8192], P('dp', 'ctx', 'tp'), may hold values from -5 to 5
- step_raw: float32 [2, 128, 4096], P('dp', 'tp', 'ctx'), may hold values from -6 to 0
- b_proj: bfloat16 [2, 4096, 1024], P('dp', 'ctx', 'tp'), may hold values from -1.796875 to 1.796875
- c_proj: bfloat16 [2, 4096, 1024], P('dp', 'ctx', 'tp'), may hold values from -1.796875 to 1.796875
- rate_log: float32 [128], P('tp'), may hold values from -25 to 0
- step_bias: float32 [128], P('tp'), may hold values from -0.5 to 0.5
- skip_gain: float32 [128], P('tp'), may hold values from 0.5 to 1.5
- norm_gain: float32 [8192], P('tp'), may hold values from 0.25 to 1.75
- ssm_grad_out: bfloat16 [2, 4096, 8192], P('dp', 'ctx', 'tp'), may hold values from -6 to 6
- queries: bfloat16 [2, 4096, 8192], P('dp', 'ctx', 'tp'), may hold values from -24 to 24
- keys: bfloat16 [2, 4096, 1024], P('dp', 'ctx', 'tp'), may hold values from -4 to 4
- values: bfloat16 [2, 4096, 1024], P('dp', 'ctx', 'tp'), may hold values from -6 to 6
- attention_output_gradient: bfloat16 [2, 4096, 8192], P('dp', 'ctx', 'tp'), may hold values from -6 to 6
- doc_lengths: int32 [2, 17], P('dp'), may hold values from 1 to 512, 4096 in all within a row
Outputs:
- grad_input: bfloat16 [2, 4096, 8192], P('dp', 'ctx', 'tp')
- grad_gate: bfloat16 [2, 4096, 8192], P('dp', 'ctx', 'tp')
- grad_raw: float32 [2, 128, 4096], P('dp', 'tp', 'ctx')
- grad_b: bfloat16 [2, 4096, 1024], P('dp', 'ctx', 'tp')
- grad_c: bfloat16 [2, 4096, 1024], P('dp', 'ctx', 'tp')
- grad_rate: float32 [128], P('tp')
- grad_skip: float32 [128], P('tp')
- grad_gain: float32 [8192], P('tp')
- grad_queries: bfloat16 [2, 4096, 8192], P('dp', 'ctx', 'tp')
- grad_keys: bfloat16 [2, 4096, 1024], P('dp', 'ctx', 'tp')
- grad_values: bfloat16 [2, 4096, 1024], P('dp', 'ctx', 'tp')
Inputs may be any that keep to these rules, and one draw needn't show every extreme that they name: `doc_lengths`: each row sums to 4096, and its largest entry is exactly 512.
All inputs are finite; a program needn't handle non-finite values.
Results may differ from a plain program's by a relative error of at most 0.007.
Values may be sent and summed in bfloat16 or wider, within the bound.
A program may use at most 128 MiB of HBM per device.

v0:
```python
import math

import jax
import jax.numpy as jnp
from jax import lax
from jax.sharding import PartitionSpec as P

HS = 128
P_SIZE = 64
NST = 128
CH = 128
HEAD_CHANNELS = 128
KEYS_PER_BLOCK = 512


precise = lax.Precision.HIGHEST
masked_score = -1e30
norm_epsilon = 1e-05


def carried_in_2(part, axis, combine, identity, reverse):
    count = lax.axis_size(axis)
    place = lax.axis_index(axis)
    ahead = count - 1 - place if reverse else place
    gathered = jax.tree.map(lambda a: lax.all_gather(a, axis), part)
    state = jax.tree.map(lambda a, e: jnp.zeros_like(a) + jnp.asarray(e, a.dtype), part, identity)

    def one(turn, state):
        source = count - 1 - turn if reverse else turn
        return combine(
            state, jax.tree.map(lambda a: lax.dynamic_index_in_dim(a, source, 0, False), gathered)
        )

    return lax.fori_loop(0, ahead, one, state)


def passed_along(shard, axis, by):
    devices = lax.axis_size(axis)
    pairs = [(i, i + by) for i in range(devices) if 0 <= i + by < devices]
    return lax.ppermute(shard, axis, pairs)


def doc_index(token_positions, doc_ends):
    return jnp.sum((token_positions[:, None] >= doc_ends[None, :]).astype(jnp.int32), axis=1)


def doc_begin(token_positions, doc_ends, lengths):
    return jnp.sum(
        jnp.where(token_positions[:, None] >= doc_ends[None, :], lengths[None, :], 0), axis=1
    )


def chain_step(earlier, later):
    return (earlier[0] * later[0], later[0][:, None, None] * earlier[1] + later[1])


def state_scan(
    inputs, step_sizes, b_rows, c_rows, decay_rates, skip_gains, document_labels, before, block_len
):
    rows_count, head_count, head_width = inputs.shape
    group_count, state_width = (b_rows.shape[1], b_rows.shape[2])
    group_heads = head_count // group_count
    block_count = rows_count // block_len
    x_blocks = inputs.reshape(block_count, block_len, group_count, group_heads, head_width)
    step_blocks = step_sizes.reshape(head_count, block_count, block_len).transpose(1, 0, 2)
    b_blocks = b_rows.reshape(block_count, block_len, group_count, state_width)
    c_blocks = c_rows.reshape(block_count, block_len, group_count, state_width)
    doc_blocks = document_labels.reshape(block_count, block_len)
    offsets = jnp.arange(block_len)
    causal = offsets[:, None] >= offsets[None, :]

    def advance(carried_in, inputs_now):
        state_now, last_doc = carried_in
        x_here, step_here, b_here, c_here, doc_here = inputs_now
        cumulative = jnp.cumsum(-decay_rates[:, None] * step_here, axis=1)
        within = (doc_here[:, None] == doc_here[None, :]) & causal
        exponent = jnp.where(
            within[None], cumulative[:, :, None] - cumulative[:, None, :], masked_score
        )
        decays = jnp.exp(exponent).reshape(group_count, group_heads, block_len, block_len)
        intersection = jnp.einsum("tgn,sgn->gts", c_here, b_here, precision=precise)
        weights = (
            decays
            * intersection[:, None]
            * step_here.reshape(group_count, group_heads, 1, block_len)
        )
        inside = jnp.einsum("gjts,sgjp->tgjp", weights, x_here, precision=precise)
        survive = jnp.where((doc_here == last_doc)[None, :], jnp.exp(cumulative), 0.0)
        survive = survive.reshape(group_count, group_heads, block_len).transpose(2, 0, 1)
        carried = (
            jnp.einsum("gjpn,tgn->tgjp", state_now, c_here, precision=precise) * survive[..., None]
        )
        outputs = (
            inside
            + carried
            + skip_gains.reshape(group_count, group_heads)[None, :, :, None] * x_here
        )
        tail_weight = (
            jnp.where(
                (doc_here == doc_here[-1])[None, :], jnp.exp(cumulative[:, -1:] - cumulative), 0.0
            )
            * step_here
        )
        injected = jnp.einsum(
            "gjs,sgjp,sgn->gjpn",
            tail_weight.reshape(group_count, group_heads, block_len),
            x_here,
            b_here,
            precision=precise,
        )
        retained = jnp.where(doc_here[-1] == last_doc, jnp.exp(cumulative[:, -1]), 0.0).reshape(
            group_count, group_heads
        )
        return ((injected + retained[:, :, None, None] * state_now, doc_here[-1]), outputs)

    initial = (jnp.zeros((group_count, group_heads, head_width, state_width), jnp.float32), before)
    (final_state, _), outputs = lax.scan(
        advance, initial, (x_blocks, step_blocks, b_blocks, c_blocks, doc_blocks)
    )
    return (
        outputs.reshape(rows_count, head_count, head_width),
        final_state.reshape(head_count, head_width, state_width),
    )


def attention_grads(
    query_row_block,
    grad_rows,
    key_value_rows,
    query_pos,
    query_docs,
    query_begin,
    key_pos,
    key_docs,
):
    scale_factor = 1.0 / math.sqrt(HEAD_CHANNELS)
    key_count = key_value_rows.shape[0]
    kv_heads = key_value_rows.shape[2]
    heads_per_group = query_row_block.shape[2]
    rows_count = query_row_block.shape[0]
    block_count = key_count // KEYS_PER_BLOCK
    kv_blocks = key_value_rows.reshape(block_count, KEYS_PER_BLOCK, 2, kv_heads, HEAD_CHANNELS)
    pos_blocks = key_pos.reshape(block_count, KEYS_PER_BLOCK)
    doc_blocks = key_docs.reshape(block_count, KEYS_PER_BLOCK)
    lowest = jnp.min(query_begin)
    highest = jnp.max(query_pos)

    def allowed_of(block_pos, block_docs):
        allowed = (
            (block_pos[None, :] <= query_pos[:, None])
            & (block_docs[None, :] == query_docs[:, None])
            & (block_pos[None, :] >= 0)
        )
        return allowed[None, None]

    def active(block_pos):
        return (block_pos[-1] >= lowest) & (block_pos[0] <= highest)

    def scores_of(block_keys, allowed):
        raw_scores = (
            jnp.einsum(
                "icge,jce->cgij", query_row_block, block_keys, preferred_element_type=jnp.float32
            )
            * scale_factor
        )
        return jnp.where(allowed, raw_scores, masked_score)

    def first_pass(running, blocks_now):
        block_kv, block_pos, block_docs = blocks_now

        def first_accumulate(running):
            top_score, total, weighted = running
            allowed = allowed_of(block_pos, block_docs)
            scores = scores_of(block_kv[:, 0], allowed)
            new_top = jnp.maximum(top_score, jnp.max(scores, axis=-1))
            expo = jnp.where(allowed, jnp.exp(scores - new_top[..., None]), 0.0)
            grad_dots = jnp.einsum(
                "icge,jce->cgij", grad_rows, block_kv[:, 1], preferred_element_type=jnp.float32
            )
            fade = jnp.exp(top_score - new_top)
            return (
                new_top,
                total * fade + jnp.sum(expo, axis=-1),
                weighted * fade + jnp.sum(expo * grad_dots, axis=-1),
            )

        def unchanged(running):
            return running

        return (lax.cond(active(block_pos), first_accumulate, unchanged, running), None)

    stat_shape = (kv_heads, heads_per_group, rows_count)
    initial = (
        jnp.full(stat_shape, masked_score, jnp.float32),
        jnp.zeros(stat_shape, jnp.float32),
        jnp.zeros(stat_shape, jnp.float32),
    )
    (top_score, total, weighted), _ = lax.scan(
        first_pass, initial, (kv_blocks, pos_blocks, doc_blocks)
    )
    log_total = top_score + jnp.log(total)
    centre = weighted / total

    def second_pass(query_gradient, blocks_now):
        block_kv, block_pos, block_docs = blocks_now

        def second_accumulate(query_gradient):
            allowed = allowed_of(block_pos, block_docs)
            scores = scores_of(block_kv[:, 0], allowed)
            probs = jnp.where(allowed, jnp.exp(scores - log_total[..., None]), 0.0)
            grad_dots = jnp.einsum(
                "icge,jce->cgij", grad_rows, block_kv[:, 1], preferred_element_type=jnp.float32
            )
            prob_low = probs.astype(jnp.bfloat16)
            score_grad = (probs * (grad_dots - centre[..., None])).astype(jnp.bfloat16)
            grad_key = (
                jnp.einsum(
                    "cgij,icge->jce",
                    score_grad,
                    query_row_block,
                    preferred_element_type=jnp.float32,
                )
                * scale_factor
            )
            grad_value = jnp.einsum(
                "cgij,icge->jce", prob_low, grad_rows, preferred_element_type=jnp.float32
            )
            query_gradient = query_gradient + jnp.einsum(
                "cgij,jce->icge", score_grad, block_kv[:, 0], preferred_element_type=jnp.float32
            )
            return (query_gradient, jnp.stack([grad_key, grad_value], axis=1))

        def skipped(query_gradient):
            return (
                query_gradient,
                jnp.zeros((KEYS_PER_BLOCK, 2, kv_heads, HEAD_CHANNELS), jnp.float32),
            )

        return lax.cond(active(block_pos), second_accumulate, skipped, query_gradient)

    query_gradient, gradient_blocks = lax.scan(
        second_pass,
        jnp.zeros((rows_count, kv_heads, heads_per_group, HEAD_CHANNELS), jnp.float32),
        (kv_blocks, pos_blocks, doc_blocks),
    )
    return (
        query_gradient * scale_factor,
        gradient_blocks.reshape(key_count, 2, kv_heads, HEAD_CHANNELS),
    )


def per_device(
    ssm_input,
    ssm_gate,
    step_raw,
    b_proj,
    c_proj,
    rate_log,
    step_bias,
    skip_gain,
    norm_gain,
    ssm_grad_out,
    queries,
    keys,
    values,
    attention_output_gradient,
    doc_lengths,
):
    tokens_here = ssm_input.shape[1]
    device_index = lax.axis_index("ctx")
    lengths = doc_lengths[0]
    doc_ends = jnp.cumsum(lengths)
    token_positions = device_index * tokens_here + jnp.arange(tokens_here, dtype=jnp.int32)
    document_labels = doc_index(token_positions, doc_ends)
    before = doc_index(token_positions[:1] - 1, doc_ends)[0]
    head_count = rate_log.shape[0]
    inputs = ssm_input[0].astype(jnp.float32).reshape(tokens_here, head_count, P_SIZE)
    b_rows = b_proj[0].astype(jnp.float32).reshape(tokens_here, -1, NST)
    c_rows = c_proj[0].astype(jnp.float32).reshape(tokens_here, -1, NST)
    raw_steps = step_raw[0]

    def local_part(inputs, raw_steps, b_rows, c_rows, rate_log, step_bias, skip_gain):
        step_sizes = jax.nn.softplus(raw_steps + step_bias[:, None])
        decay_rates = jnp.exp(rate_log)
        mixed_zero, local_state = state_scan(
            inputs, step_sizes, b_rows, c_rows, decay_rates, skip_gain, document_labels, before, CH
        )
        decay_total = jnp.where(
            document_labels[-1] == before, jnp.exp(-decay_rates * jnp.sum(step_sizes, axis=1)), 0.0
        )
        return (mixed_zero, local_state, decay_total)

    def entry_part(raw_steps, c_rows, rate_log, step_bias, entry_state):
        step_sizes = jax.nn.softplus(raw_steps + step_bias[:, None])
        decay_rates = jnp.exp(rate_log)
        cumulative = jnp.cumsum(-decay_rates[:, None] * step_sizes, axis=1)
        survive = jnp.where((document_labels == before)[None, :], jnp.exp(cumulative), 0.0)
        group_count = c_rows.shape[1]
        group_heads = head_count // group_count
        survive = survive.reshape(group_count, group_heads, tokens_here).transpose(2, 0, 1)
        carried = (
            jnp.einsum(
                "gjpn,tgn->tgjp",
                entry_state.reshape(group_count, group_heads, P_SIZE, NST),
                c_rows,
                precision=precise,
            )
            * survive[..., None]
        )
        return carried.reshape(tokens_here, head_count, P_SIZE)

    (mixed_zero, local_state, decay_total), pull_local = jax.vjp(
        local_part, inputs, raw_steps, b_rows, c_rows, rate_log, step_bias, skip_gain
    )
    identity = (jnp.ones((head_count,), jnp.float32), jnp.zeros_like(local_state))
    _, entry_state = carried_in_2((decay_total, local_state), "ctx", chain_step, identity, False)
    mixed_entry, pull_entry = jax.vjp(
        entry_part, raw_steps, c_rows, rate_log, step_bias, entry_state
    )
    mixed = (mixed_zero + mixed_entry).reshape(tokens_here, head_count * P_SIZE)
    gate_values = ssm_gate[0].astype(jnp.float32)
    sigma = jax.nn.sigmoid(gate_values)
    activation = gate_values * sigma
    gated = mixed * activation
    out_grad = ssm_grad_out[0].astype(jnp.float32)
    scaled_grad = out_grad * norm_gain[None, :]
    square_sum, cross_sum = lax.psum(
        (jnp.sum(gated * gated, axis=1), jnp.sum(gated * scaled_grad, axis=1)), "tp"
    )
    full_width = HS * P_SIZE
    factor = lax.rsqrt(square_sum / full_width + norm_epsilon)
    gated_grad = (
        factor[:, None] * scaled_grad
        - gated * (factor * factor * factor * cross_sum / full_width)[:, None]
    )
    gain_grad = jnp.sum(out_grad * gated * factor[:, None], axis=0)
    gate_grad = gated_grad * mixed * sigma * (1.0 + gate_values * (1.0 - sigma))
    mixed_grad = (gated_grad * activation).reshape(tokens_here, head_count, P_SIZE)
    entry_grads = pull_entry(mixed_grad)
    _, next_grad = carried_in_2((decay_total, entry_grads[4]), "ctx", chain_step, identity, True)
    decay_grad = jnp.sum(next_grad * entry_state, axis=(1, 2))
    local_grads = pull_local((mixed_grad, next_grad, decay_grad))
    rate_grad = local_grads[4] + entry_grads[2]
    rate_sum, skip_sum, gain_sum = lax.psum((rate_grad, local_grads[6], gain_grad), ("ctx", "dp"))
    grad_input = local_grads[0].reshape(tokens_here, head_count * P_SIZE)[None].astype(jnp.bfloat16)
    grad_gate = gate_grad[None].astype(jnp.bfloat16)
    grad_raw = (local_grads[1] + entry_grads[0])[None]
    grad_b = local_grads[2].reshape(tokens_here, -1)[None].astype(jnp.bfloat16)
    grad_c = (local_grads[3] + entry_grads[1]).reshape(tokens_here, -1)[None].astype(jnp.bfloat16)
    kv_heads = keys.shape[2] // HEAD_CHANNELS
    query_row_block = queries[0].reshape(tokens_here, kv_heads, -1, HEAD_CHANNELS)
    grad_rows = attention_output_gradient[0].reshape(tokens_here, kv_heads, -1, HEAD_CHANNELS)
    query_begin = doc_begin(token_positions, doc_ends, lengths)
    pair_local = jnp.concatenate([keys[0], values[0]], axis=1)
    reach = min(4, lax.axis_size("ctx") // 2)
    slots = 2 * reach
    pieces = [pair_local]
    carry_piece = pair_local
    for hop_index in range(reach):
        carry_piece = passed_along(carry_piece, "ctx", 1)
        pieces.insert(0, carry_piece)
    padding = jnp.zeros(((slots - reach - 1) * tokens_here, pair_local.shape[1]), pair_local.dtype)
    window = jnp.concatenate([padding] + pieces, axis=0)
    first_key = (device_index + 1 - slots) * tokens_here
    key_count = window.shape[0]
    key_pos = first_key + jnp.arange(key_count, dtype=jnp.int32)
    key_docs = doc_index(key_pos, doc_ends)
    query_gradient, gradient_pairs = attention_grads(
        query_row_block,
        grad_rows,
        window.reshape(key_count, 2, kv_heads, HEAD_CHANNELS),
        token_positions,
        document_labels,
        query_begin,
        key_pos,
        key_docs,
    )
    gradient_pairs = gradient_pairs.reshape(key_count, 2 * kv_heads * HEAD_CHANNELS)
    slot_rows = gradient_pairs.reshape(slots, tokens_here, -1)
    running_sum = slot_rows[slots - 1 - reach]
    for hop_index in range(reach):
        running_sum = (
            passed_along(running_sum.astype(jnp.bfloat16), "ctx", -1).astype(running_sum.dtype)
            + slot_rows[slots - reach + hop_index]
        )
    grad_queries = query_gradient.reshape(tokens_here, -1)[None].astype(jnp.bfloat16)
    grad_keys = running_sum[:, : kv_heads * HEAD_CHANNELS][None].astype(jnp.bfloat16)
    grad_values = running_sum[:, kv_heads * HEAD_CHANNELS :][None].astype(jnp.bfloat16)
    return (
        grad_input,
        grad_gate,
        grad_raw,
        grad_b,
        grad_c,
        rate_sum,
        skip_sum,
        gain_sum,
        grad_queries,
        grad_keys,
        grad_values,
    )


def solution(mesh):
    placed = (
        P("dp", "ctx", "tp"),
        P("dp", "ctx", "tp"),
        P("dp", "tp", "ctx"),
        P("dp", "ctx", "tp"),
        P("dp", "ctx", "tp"),
        P("tp"),
        P("tp"),
        P("tp"),
        P("tp"),
        P("dp", "ctx", "tp"),
        P("dp", "ctx", "tp"),
        P("dp", "ctx", "tp"),
        P("dp", "ctx", "tp"),
        P("dp", "ctx", "tp"),
        P("dp", None),
    )
    return jax.shard_map(
        per_device,
        mesh=mesh,
        in_specs=placed,
        out_specs=(
            P("dp", "ctx", "tp"),
            P("dp", "ctx", "tp"),
            P("dp", "tp", "ctx"),
            P("dp", "ctx", "tp"),
            P("dp", "ctx", "tp"),
            P("tp"),
            P("tp"),
            P("tp"),
            P("dp", "ctx", "tp"),
            P("dp", "ctx", "tp"),
            P("dp", "ctx", "tp"),
        ),
        check_vma=False,
    )
```

profile of v0, /device:TPU:1, one launch (start us, length us, event | category | flops | bytes accessed | tf_op | source)
XLA Modules:
  0.0 778.8 jit_solution(7230560174957064598)
XLA Ops:
  19.0 1.6 convolution_add_fusion
  26.7 65.1 %all-reduce.2 = f32[1024]{0:T(1024)S(1)} all-reduce(f32[1024]{0:T(1024)S(1)} %fusion.134), channel_id=2, replica_groups=mesh['ctx'=32,'dp'=2,'tp'=4] {'ctx'}, use_global_device_ids=true, to_apply=%add.2 | all-reduce | flops 1024 | bytes 8192
  92.4 1.6 convolution_bitcast_fusion.4
  93.9 164.6 %all-gather.4.cloned.1.call-done = f32[32,32,64,128]{3,2,1,0:T(8,128)} async-done(((f32[1,32,64,128]{3,2,1,0:T(8,128)}), f32[32,32,64,128]{3,2,1,0:T(8,128)}) %all-gather.4.cloned.1.call-update) | async-done | bytes 33554448 | tf_op jit(solution)/shard_map/all_gather | solution.py:25
  260.2 3.8 multiply_reduce_fusion.7
  264.0 8.5 %all-reduce.4 = (f32[128]{0:T(128)S(1)}, f32[128]{0:T(128)S(1)}) all-reduce(f32[128]{0:T(128)S(1)} %get-tuple-element.1083, f32[128]{0:T(128)S(1)} %get-tuple-element.1082), channel_id=1, replica_groups=mesh['ctx'=32,'dp'=2,'tp'=4] {'tp'}, use_global_device_ids=true, to_apply=%region_10.12 | all-reduce | flops 256 | bytes 2048 | tf_op jit(solution)/shard_map/psum | solution.py:327
  272.5 2.0 subtract_multiply_fusion
  275.5 1.6 fusion.86
  277.2 3.0 collective-permute-start
  280.2 1.9 collective-permute-done
  282.1 4.7 collective-permute-start.1
  286.8 1.9 collective-permute-done.1
  288.7 6.5 collective-permute-start.2
  296.6 4.5 collective-permute-start.3
  303.7 1.6 constant_dynamic-update-slice_fusion.4
  305.3 1.6 constant_dynamic-update-slice_fusion.3
  306.9 1.6 constant_dynamic-update-slice_fusion.2
  308.4 1.6 constant_dynamic-update-slice_fusion.1
  310.0 1.5 constant_dynamic-update-slice_fusion
  311.5 1.8 reshape_reshape.2
  314.5 11.1 %while.20 = (s32[]{:T(128)}, f32[2,8,128]{2,1,0:T(8,128)S(1)}, f32[2,8,128]{2,1,0:T(8,128)S(1)}, f32[2,8,128]{2,1,0:T(8,128)S(1)}, s32[2,512]{1,0:T(2,128)S(1)},...) while((s32[]{:T(128)}, f32[2,8,128]{2,1,0:T(8,128)S(1)}, ...), condition=%wide.region_41.43_spmd.clone, body=%wide.region_35.42_spmd.clone.sunk | while | flops 551819904 | bytes 15632259 | solution.py:198
  320.9 4.6 conditional.6
  327.3 17.0 %while.40 = (s32[]{:T(128)}, f32[128,2,8,128]{3,0,2,1:T(8,128)}, f32[2,512,2,2,128]{4,3,2,1,0:T(2,128)}, s32[2,512]{1,0:T(2,128)S(1)}, s32[]{:T(128)}, /*index=5...) while((s32[]{:T(128)}, f32[128,2,8,128]{3,0,2,1:T(8,128)}, ...), condition=%wide.region_45.47_spmd.clone, body=%wide.region_42.46_spmd.clone.sunk | while | flops 1355678336 | bytes 38807992 | solution.py:241
  330.6 1.8 copy_dynamic-update-slice_fusion.2
  335.6 6.9 conditional.7
  337.8 1.5 fusion.9
  342.5 1.8 copy_dynamic-update-slice_fusion.2
  344.3 4.0 reshape_reshape_reshape.3
  350.7 8.5 %collective-permute-done.4 = bf16[128,512]{1,0:T(8,128)(2,1)S(1)} collective-permute-done((bf16[128,512]{1,0:T(8,128)(2,1)S(1)}, bf16[128,512]{1,0:T(8,128)(2,1)S(1)}, u32[]{:S(2)}, u32[]{:S(2)}) %collective-permute-start.4) | collective-permute-done | bytes 131104 | tf_op jit(solution)/shard_map/ppermute | solution.py:40
  361.4 9.2 %collective-permute-done.5 = bf16[128,512]{1,0:T(8,128)(2,1)S(1)} collective-permute-done((bf16[128,512]{1,0:T(8,128)(2,1)S(1)}, bf16[128,512]{1,0:T(8,128)(2,1)S(1)}, u32[]{:S(2)}, u32[]{:S(2)}) %collective-permute-start.5) | collective-permute-done | bytes 131104 | tf_op jit(solution)/shard_map/ppermute | solution.py:40
  372.9 8.8 %collective-permute-done.6 = bf16[128,512]{1,0:T(8,128)(2,1)S(1)} collective-permute-done((bf16[128,512]{1,0:T(8,128)(2,1)S(1)}, bf16[128,512]{1,0:T(8,128)(2,1)S(1)}, u32[]{:S(2)}, u32[]{:S(2)}) %collective-permute-start.6) | collective-permute-done | bytes 131104 | tf_op jit(solution)/shard_map/ppermute | solution.py:40
  381.8 1.6 fusion.114
  383.4 1.5 collective-permute-start.7
  386.1 2.1 convert_element_type.225
  392.6 5.0 fusion.56
  397.5 1.4 copy.218
  403.0 1.8 convolution_bitcast_fusion.6
  407.2 2.8 fusion.98
  410.1 1.5 fusion.73
  411.6 149.3 %all-gather.6.cloned.1.call-done = f32[32,32,64,128]{3,2,1,0:T(8,128)} async-done(((f32[1,32,64,128]{3,2,1,0:T(8,128)}), f32[32,32,64,128]{3,2,1,0:T(8,128)}) %all-gather.6.cloned.1.call-update) | async-done | bytes 33554448 | tf_op jit(solution)/shard_map/all_gather | solution.py:25
  561.0 67.3 %while.19 = (s32[]{:T(128)}, f32[32,64,128]{2,1,0:T(8,128)S(1)}, s32[]{:T(128)}, f32[32,32]{1,0:T(8,128)}, f32[32,32,64,128]{3,2,1,0:T(8,128)}, /*index=5*/s32[]{:T(128)}, s32[]{:T(128)}, s32[]{:T(128)}, s32[]{:T(128)}) while((s32[]{:T(128)}, f32[32,64,128]{2,1,0:T(8,128)S(1)}, s32[]{:T(128)}, f32[32,32]{1,0:T(8,128)}, ...), condition=%wide.region_12.14_spmd, body=%wide.region_11.13_spmd.sunk | while | flops 524294 | bytes 3146267 | solution.py:34
  566.0 1.4 bitcast_add_fusion.6
  568.2 1.4 bitcast_add_fusion.6
  576.8 1.4 bitcast_add_fusion.6
  629.7 2.3 fusion.62
  632.0 1.8 fusion.57
  633.9 2.4 fusion.51
  642.8 128.9 %all-reduce.3 = (f32[32]{0:T(128)}, f32[32]{0:T(128)}, f32[2048]{0:T(1024)}) all-reduce(f32[32]{0:T(128)S(1)} %add_multiply_fusion, f32[32]{0:T(128)S(1)} %reshape.952, f32[2048]{0:T(1024)S(1)} %copy-done.39), channel_id=1, replica_groups=mesh['ctx'=32,'dp'=2,'tp'=4] {'ctx','dp'}, use_global_device_ids=true, to_apply=%region_26.28 | all-reduce | flops 2112 | bytes 16896 | tf_op jit(solution)/shard_map/psum | solution.py:344
  (330 shorter events, 125.1 us)
Async XLA Ops:
  7.2 251.4 %all-gather.4.cloned.1.call-start = ((), (), s32[]{:S(2)}) async-start(), calls=%async_computation | async-start | bytes 34603008 | tf_op jit(solution)/shard_map/all_gather | solution.py:25
  13.8 6.9 copy-start.43
  13.8 6.9 copy-start.51
  15.3 6.2 copy-start.9
  16.6 242.7 %copy-start.7 = (bf16[1,128,2048]{1,2,0:T(8,128)(2,1)}, bf16[1,128,2048]{1,2,0:T(8,128)(2,1)S(1)}, u32[]{:S(2)}) copy-start(bf16[1,128,2048]{1,2,0:T(8,128)(2,1)S(1)} %copy.200) | copy-start | bytes 1572868
  17.4 9.1 %copy-start.47 = (f32[32]{0:T(128)}, f32[32]{0:T(128)S(1)}, u32[]{:S(2)}) copy-start(f32[32]{0:T(128)S(1)} %get-tuple-element.1189) | copy-start | bytes 388
  17.8 374.8 %copy-start.27 = (f32[32,128]{1,0:T(8,128)}, f32[32,128]{1,0:T(8,128)S(1)}, u32[]{:S(2)}) copy-start(f32[32,128]{1,0:T(8,128)S(1)} %reduce_window_sum.45) | copy-start | bytes 49156
  18.0 241.3 %copy-start.34 = (f32[32,128]{1,0:T(8,128)}, f32[32,128]{1,0:T(8,128)S(1)}, u32[]{:S(2)}) copy-start(f32[32,128]{1,0:T(8,128)S(1)} %copy.199) | copy-start | bytes 49156
  20.7 4.6 copy-start.65
  20.7 5.9 copy-start.55
  20.7 71.1 %copy-start.33 = (bf16[1,128,256]{2,1,0:T(8,128)(2,1)S(1)}, bf16[1,128,256]{2,1,0:T(8,128)(2,1)}, u32[]{:S(2)}) copy-start(bf16[1,128,256]{2,1,0:T(8,128)(2,1)} %param.32) | copy-start | bytes 196612
  20.7 71.2 %copy-start.62 = (f32[32]{0:T(128)S(1)}, f32[32]{0:T(128)}, u32[]{:S(2)}) copy-start(f32[32]{0:T(128)} %param.35) | copy-start | bytes 388
  20.7 540.1 %all-gather.6.cloned.1.call-start = ((), (), s32[]{:S(2)}) async-start(), calls=%async_computation.1 | async-start | bytes 34603008 | tf_op jit(solution)/shard_map/all_gather | solution.py:25
  91.9 167.4 %copy-start.63 = (f32[2,16]{1,0:T(2,128)}, f32[2,16]{1,0:T(2,128)S(1)}, u32[]{:S(2)}) copy-start(f32[2,16]{1,0:T(2,128)S(1)} %mul.573) | copy-start | bytes 388
  92.1 167.2 %copy-start.41 = (pred[128,128]{1,0:T(8,128)(4,1)}, pred[128,128]{1,0:T(8,128)(4,1)S(1)}, u32[]{:S(2)}) copy-start(pred[128,128]{1,0:T(8,128)(4,1)S(1)} %fusion.125) | copy-start | bytes 49156
  92.4 167.0 %copy-start.29 = (f32[2,128,128]{2,1,0:T(8,128)}, f32[2,128,128]{2,1,0:T(8,128)S(1)}, u32[]{:S(2)}) copy-start(f32[2,128,128]{2,1,0:T(8,128)S(1)} %fusion.148) | copy-start | bytes 393220
  258.7 5.3 copy-start.40
  259.3 4.7 copy-start.15
  264.0 10.5 %copy-start.5 = (f32[128,2,16,64]{0,3,2,1:T(8,128)}, f32[128,2,16,64]{0,3,2,1:T(8,128)S(1)}, u32[]{:S(2)}) copy-start(f32[128,2,16,64]{0,3,2,1:T(8,128)S(1)} %get-tuple-element.1201) | copy-start | bytes 3145732
  275.5 25.6 %copy-start.18 = (bf16[1,128,2048]{2,1,0:T(8,128)(2,1)S(1)}, bf16[1,128,2048]{2,1,0:T(8,128)(2,1)}, u32[]{:S(2)}) copy-start(bf16[1,128,2048]{2,1,0:T(8,128)(2,1)} %param.38) | copy-start | bytes 1572868
  277.1 24.6 %copy-start.19 = (bf16[1,128,2048]{2,1,0:T(8,128)(2,1)S(1)}, bf16[1,128,2048]{2,1,0:T(8,128)(2,1)}, u32[]{:S(2)}) copy-start(bf16[1,128,2048]{2,1,0:T(8,128)(2,1)} %param.41) | copy-start | bytes 1572868
  277.2 5.0 collective-permute-start
  282.1 19.0 %copy-start.31 = (bf16[128,512]{1,0:T(8,128)(2,1)}, bf16[128,512]{1,0:T(8,128)(2,1)S(1)}, u32[]{:S(2)}) copy-start(bf16[128,512]{1,0:T(8,128)(2,1)S(1)} %collective-permute-done) | copy-start | bytes 393220
  282.1 6.6 collective-permute-start.1
  288.7 12.4 %copy-start.32 = (bf16[128,512]{1,0:T(8,128)(2,1)}, bf16[128,512]{1,0:T(8,128)(2,1)S(1)}, u32[]{:S(2)}) copy-start(bf16[128,512]{1,0:T(8,128)(2,1)S(1)} %collective-permute-done.1) | copy-start | bytes 393220
  288.7 7.8 %collective-permute-start.2 = (bf16[128,512]{1,0:T(8,128)(2,1)S(1)}, bf16[128,512]{1,0:T(8,128)(2,1)}, u32[]{:S(2)}, u32[]{:S(2)}) collective-permute-start(bf16[128,512]{1,0:T(8,128)(2,1)S(1)} %collective-permute-done.1), channel_id=1, source_target_pairs={{0,8},{8,16},{16,24},{24,32},{32,40},{40,48},{48,56},{56,64},{64,7... | collective-permute-start | bytes 393224 | tf_op jit(solution)/shard_map/ppermute | solution.py:40
  296.6 7.2 collective-permute-start.3
  344.3 40.5 %copy-start.2 = (f32[128,2,8,128]{3,0,2,1:T(8,128)S(1)}, f32[128,2,8,128]{3,0,2,1:T(8,128)}, u32[]{:S(2)}) copy-start(f32[128,2,8,128]{3,0,2,1:T(8,128)} %get-tuple-element.804) | copy-start | bytes 3145732
  349.4 9.8 %collective-permute-start.4 = (bf16[128,512]{1,0:T(8,128)(2,1)S(1)}, bf16[128,512]{1,0:T(8,128)(2,1)S(1)}, u32[]{:S(2)}, u32[]{:S(2)}) collective-permute-start(bf16[128,512]{1,0:T(8,128)(2,1)S(1)} %fusion.120), channel_id=1, source_target_pairs={{8,0},{16,8},{24,16},{32,24},{40,32},{48,40},{56,48},{64,56},{72,6... | collective-permute-start | bytes 393224 | tf_op jit(solution)/shard_map/ppermute | solution.py:40
  360.1 10.5 %collective-permute-start.5 = (bf16[128,512]{1,0:T(8,128)(2,1)S(1)}, bf16[128,512]{1,0:T(8,128)(2,1)S(1)}, u32[]{:S(2)}, u32[]{:S(2)}) collective-permute-start(bf16[128,512]{1,0:T(8,128)(2,1)S(1)} %fusion.118), channel_id=1, source_target_pairs={{8,0},{16,8},{24,16},{32,24},{40,32},{48,40},{56,48},{64,56},{72,6... | collective-permute-start | bytes 393224 | tf_op jit(solution)/shard_map/ppermute | solution.py:40
  371.6 10.1 %collective-permute-start.6 = (bf16[128,512]{1,0:T(8,128)(2,1)S(1)}, bf16[128,512]{1,0:T(8,128)(2,1)S(1)}, u32[]{:S(2)}, u32[]{:S(2)}) collective-permute-start(bf16[128,512]{1,0:T(8,128)(2,1)S(1)} %fusion.116), channel_id=1, source_target_pairs={{8,0},{16,8},{24,16},{32,24},{40,32},{48,40},{56,48},{64,56},{72,6... | collective-permute-start | bytes 393224 | tf_op jit(solution)/shard_map/ppermute | solution.py:40
  383.4 6.0 collective-permute-start.7
  385.0 6.2 copy-start.6
  386.1 6.4 copy-start.4
  386.1 6.4 copy-start.35
  405.9 4.1 copy-start.54
  629.7 4.2 copy-start.28
  629.7 4.2 copy-start.30
  629.7 4.2 copy-start.36
  629.7 4.2 copy-start.42
  629.7 4.2 copy-start.64
  636.4 4.5 copy-start.48
  636.4 4.5 copy-start.56
  636.4 4.5 copy-start.57
  636.4 4.5 copy-start.24
  636.4 4.5 copy-start.59
  636.4 5.3 copy-start.21
  636.5 6.4 copy-start.39
  (28 other events, 70.6 us)
Sparse Core Ops, SparseCore 0:
  20.8 237.6 all-gather.3
  277.3 283.5 all-gather.5
where the time goes:
time: 788 us; the launch traced here: 779 us
  waiting for transfers between devices  347 us (44%)
  blocking collectives  202 us (26%)
  local copies, waits for them, and re-layouts  72.8 us (9%)
  other arithmetic  70.7 us (9%)
  matrix products  31.7 us (4%)
  starting transfers between devices  24.2 us (3%)
  between operations  18.5 us (2%)
  loops' own time  11.9 us (2%)
    all_gather x2, waiting for transfers between devices, carried_in_2(): gathered = jax.tree.map(lambda a: lax.all_gather(a, axis), part)  314 us
    psum x1, blocking collectives, per_device(): lax.psum((rate_grad, local_grads[6], gain_grad), ('ctx', 'dp'))  129 us
    unnamed x1, blocking collectives  65.1 us
    add x31, other arithmetic, chain_step(): later[0][:, None, None] * earlier[1] + later[1]  44.6 us
    ppermute x8, waiting for transfers between devices, passed_along(): return lax.ppermute(shard, axis, pairs)  32.7 us
    ppermute x8, starting transfers between devices, passed_along(): return lax.ppermute(shard, axis, pairs)  24.1 us
    mul x31, local copies, waits for them, and re-layouts, chain_step(): later[0][:, None, None] * earlier[1] + later[1]  21.6 us
    unnamed x144, local copies, waits for them, and re-layouts  17.9 us
  transfers between devices with their start and end apart: 10, of which 9 were waited for; matrix products, arithmetic and copies ran while one was open for 9% of the time, Pallas kernels for 0%

commit v1 on v0

v1 whole, which is shorter than its diff:
```python
import jax
import jax.numpy as jnp
from jax import lax
from jax.experimental import pallas as pl
from jax.experimental.pallas import tpu as pltpu
from jax.sharding import PartitionSpec as P

MESH = pl.DeviceIdType.MESH
F32 = jnp.float32
BF16 = jnp.bfloat16
HIGH = lax.Precision.HIGHEST

TOKENS = 128
WIDE = 64
REACH = 4
CHUNK = 256
KV = 2
NORM_WIDTH = 8192
EPSILON = 1e-05
MASKED = -1e30
SCALE = 128.0**-0.5
Z_SIZE = 8
X_SIZE = 4
CORES = 2
TP_SIZE = 4


def dot(a, b, dims, precision=None):
    return lax.dot_general(
        a, b, (dims, ((), ())), precision=precision, preferred_element_type=F32
    )


def nn(a, b, precision=None):
    return dot(a, b, ((1,), (0,)), precision)


def nt(a, b, precision=None):
    return dot(a, b, ((1,), (1,)), precision)


def tn(a, b, precision=None):
    return dot(a, b, ((0,), (0,)), precision)


def iota(shape, axis):
    return lax.broadcasted_iota(jnp.int32, shape, axis)


def lanes(start, size):
    return pl.ds(pl.multiple_of(start, size), size)


def column(row):
    size = row.shape[1]
    on_diagonal = iota((size, size), 0) == iota((size, size), 1)
    return jnp.sum(jnp.where(on_diagonal, row, 0.0), axis=1, keepdims=True)


def turned(row):
    return jnp.transpose(jnp.broadcast_to(row, (TOKENS, TOKENS)))


def twice(a):
    return jnp.concatenate([a, a], axis=1)


def folded(a):
    return a[:, :TOKENS] + a[:, TOKENS:]


def kernel(
    lens, x, gate, raw, b, c, rate_log, bias, skip, gain, dout, q, k, v, do,
    gx, ggate, graw, gb, gc, grate, gskip, ggain, gq, gk, gv,
    ls, w, mixed, carried, dy, dxin, sve, tse, rows, marks, heads,
    gram, dgram, loc, dsl, fsend, frecv, bsend, brecv, kw, vw, kall, vall,
    dacc, dsend, drecv, tsum, tmsg, tbuf, cols, dc, db, hsum, zmsg, zbuf, xmsg, xbuf,
    fss, frs, bss, brs, kss, krs, dss, drs, tss, trs, zss, zrs, xss, xrs,
):
    i = lax.axis_index("ctx")
    core = lax.axis_index("dp")
    tp = lax.axis_index("tp")
    count = Z_SIZE * X_SIZE
    right = lax.rem(i + 1, count)
    left = lax.rem(i + count - 1, count)
    z = lax.rem(i, Z_SIZE)
    xi = i // Z_SIZE
    xc = xi * CORES + core
    z_peers = [xi * Z_SIZE + lax.rem(z + n, Z_SIZE) for n in range(1, Z_SIZE)]
    xc_peers = [lax.rem(xc + n, X_SIZE * CORES) for n in range(1, X_SIZE * CORES)]
    xc_ids = [{"ctx": (p // CORES) * Z_SIZE + z, "dp": lax.rem(p, CORES)} for p in xc_peers]
    tp_peers = [lax.rem(tp + n, TP_SIZE) for n in range(1, TP_SIZE)]
    n_heads = raw.shape[0]
    channels = x.shape[1]
    groups = b.shape[1] // TOKENS
    pairs = n_heads // 2 // groups

    barrier = pltpu.get_barrier_semaphore()
    greeted = (
        [{"ctx": left}, {"ctx": right}]
        + [{"tp": p} for p in tp_peers]
        + [{"ctx": p} for p in z_peers]
        + xc_ids
    )
    for device in greeted:
        pl.semaphore_signal(barrier, inc=1, device_id=device, device_id_type=MESH)
    pl.semaphore_wait(barrier, len(greeted))

    def remote(source, target, send, recv, device):
        return pltpu.make_async_remote_copy(
            src_ref=source,
            dst_ref=target,
            send_sem=send,
            recv_sem=recv,
            device_id=device,
            device_id_type=MESH,
        )

    def kv_copies(hop):
        slot = REACH - 1 - hop
        k_from = k if hop == 0 else kw.at[slot + 1]
        v_from = v if hop == 0 else vw.at[slot + 1]
        to = {"ctx": right}
        return (
            remote(k_from, kw.at[slot], kss.at[0, hop], krs.at[0, hop], to),
            remote(v_from, vw.at[slot], kss.at[1, hop], krs.at[1, hop], to),
        )

    def kv_start(hop):
        for copy in kv_copies(hop):
            copy.start()

    def kv_wait(hop):
        for copy in kv_copies(hop):
            copy.wait_recv()

    kv_start(0)

    base = i * TOKENS
    position = iota((8, TOKENS), 1) + base
    begin = jnp.zeros((8, TOKENS), jnp.int32)
    end = jnp.int32(0)
    for d in range(lens.shape[1]):
        end = end + lens[0, d]
        begin = begin + jnp.where(position >= end, lens[0, d], 0)
    begin_row = (begin - base)[0:1]
    begin_last = begin_row[:, TOKENS - 1 :]
    begin_col = turned(begin_row.astype(F32))
    row_id = iota((TOKENS, TOKENS), 0)
    lane_id = iota((TOKENS, TOKENS), 1)
    within = (lane_id <= row_id) & (lane_id.astype(F32) >= begin_col)
    up_to = (row_id <= lane_id).astype(F32)

    shifted = raw[...] + column(bias[...])
    step = jax.nn.softplus(shifted)
    rate = jnp.exp(column(rate_log[...]))
    decay = -rate * step
    cum = nn(decay, up_to, HIGH)
    cum_end = cum[:, TOKENS - 1 :]
    survive = jnp.where(begin_row < 0, jnp.exp(cum), 0.0)
    tail = jnp.where(iota((1, TOKENS), 1) >= begin_last, jnp.exp(cum_end - cum), 0.0)
    whole = jnp.where(begin_last < 0, jnp.exp(cum_end), 0.0)
    heads[0] = step
    heads[1] = cum
    heads[2] = tail
    mark = iota((n_heads, channels), 1) // WIDE == iota((n_heads, channels), 0)
    marks[...] = mark.astype(BF16)
    both = jnp.concatenate([marks[...], marks[...]], axis=0)

    def expand(a):
        high = a.astype(BF16)
        low = (a - high.astype(F32)).astype(BF16)
        return tn(jnp.concatenate([high, low], axis=0), both)

    tse[...] = expand(tail * step)
    rows[0:1] = jnp.sum(jnp.where(mark, whole, 0.0), axis=0, keepdims=True)

    def group(a, g):
        return a[:, g * TOKENS : (g + 1) * TOKENS]

    def local_state(ch, g):
        part = lanes(ch * CHUNK, CHUNK)
        inputs = (x[:, part].astype(F32) * tse[:, part]).astype(BF16)
        loc[ch] = tn(group(b, g), inputs)

    def f_chunk(stage, g):
        return g * 4 + lax.rem(stage + 4 * count - i, 4)

    def b_chunk(stage, g):
        return g * 4 + lax.rem(stage + i, 4)

    def chain(send, recv, ss, rs, device):
        def copy(leg, ch, to):
            return remote(send.at[leg, ch], recv.at[to, ch], ss.at[leg, ch], rs.at[to, ch], device)

        return copy

    f_copy = chain(fsend, frecv, fss, frs, {"ctx": right})
    b_copy = chain(bsend, brecv, bss, brs, {"ctx": left})

    def leg_a(copy, send, recv, own, ch, stage):
        value = own[ch]
        if stage > 0:
            copy(0, ch, 0).wait_recv()
            value = value + rows[0:1, lanes(ch * CHUNK, CHUNK)] * recv[0, ch].astype(F32)
        send[0, ch] = value.astype(BF16)
        copy(0, ch, 1 if stage == 3 else 0).start()

    def leg_b(copy, send, recv, own, ch, stage):
        copy(1, ch, 1).wait_recv()
        if stage < 3:
            value = own[ch] + rows[0:1, lanes(ch * CHUNK, CHUNK)] * recv[1, ch].astype(F32)
            send[1, ch] = value.astype(BF16)
            copy(1, ch, 1).start()

    def f_leg_a(stage):
        for g in range(groups):
            leg_a(f_copy, fsend, frecv, loc, f_chunk(stage, g), stage)

    def b_leg_a(stage):
        for g in range(groups):
            leg_a(b_copy, bsend, brecv, dsl, b_chunk(stage, g), stage)

    for g in range(groups):
        local_state(f_chunk(0, g), g)
    f_leg_a(0)
    for stage in range(1, 4):
        for g in range(groups):
            local_state(f_chunk(stage, g), g)
    sve[...] = expand(survive)
    rows[1:2] = jnp.sum(jnp.where(mark, column(skip[...]), 0.0), axis=0, keepdims=True)
    for g in range(groups):
        gram[g] = nt(group(c, g), group(b, g))

    left_half = iota((1, TOKENS), 1) < WIDE

    def inside_pair(g):
        def body(n, _):
            pair = g * pairs + n
            part = lanes(pair * TOKENS, TOKENS)
            for e in range(2):
                h = pair * 2 + e
                cum_row = heads[1, pl.ds(h, 1), :]
                gap = jnp.where(within, turned(cum_row) - cum_row, MASKED)
                scaled = jnp.exp(gap) * heads[0, pl.ds(h, 1), :]
                ls[h] = scaled.astype(BF16)
                w[h] = (scaled * gram[g]).astype(BF16)
            x_part = x[:, part]
            product = nn(w[pl.ds(pair * 2, 2)].reshape(2 * TOKENS, TOKENS), x_part)
            inside = jnp.where(left_half, product[:TOKENS], product[TOKENS:])
            mixed[:, part] = inside + rows[1:2, part] * x_part.astype(F32)
            return 0

        lax.fori_loop(0, pairs, body, 0)

    def attention(kv, first, last):
        key = kall[kv]
        value = vall[kv]
        window = (REACH + 1) * TOKENS
        key_at = iota((window, 2 * TOKENS), 0) - REACH * TOKENS
        query_at = twice(iota((1, TOKENS), 1))
        allowed = (key_at <= query_at) & (key_at >= twice(begin_row))

        def body(n, _):
            offset = (kv * 4 + n) * 2 * TOKENS
            part = lanes(offset, 2 * TOKENS)
            q_two = q[:, part]
            do_two = do[:, part]
            query = jnp.concatenate([q_two[:, :TOKENS], q_two[:, TOKENS:]], axis=0)
            cotangent = jnp.concatenate([do_two[:, :TOKENS], do_two[:, TOKENS:]], axis=0)
            score = jnp.where(allowed, nt(key, query) * SCALE, MASKED)
            top = jnp.max(score, axis=0, keepdims=True)
            weight = jnp.exp(score - top)
            total = jnp.sum(weight, axis=0, keepdims=True)
            prob = weight * (1.0 / total)
            reply = nt(value, cotangent)
            centre = jnp.sum(prob * reply, axis=0, keepdims=True)
            score_grad = (prob * (reply - centre)).astype(BF16)
            query_grad = (tn(score_grad, key) * SCALE).astype(BF16)
            gq[:, part] = jnp.concatenate([query_grad[:TOKENS], query_grad[TOKENS:]], axis=1)
            dacc[kv, :, 0:TOKENS] += nn(score_grad, query) * SCALE
            dacc[kv, :, TOKENS : 2 * TOKENS] += nn(prob.astype(BF16), cotangent)
            return 0

        lax.fori_loop(first, last, body, 0)

    def d_copy(kv, hop):
        return remote(
            dsend.at[kv, hop], drecv.at[kv, hop], dss.at[kv, hop], drs.at[kv, hop], {"ctx": left}
        )

    def d_hop(kv, hop):
        own = dacc[kv, hop * TOKENS : (hop + 1) * TOKENS]
        if hop > 0:
            d_copy(kv, hop - 1).wait_recv()
            own = own + drecv[kv, hop - 1].astype(F32)
        if hop < REACH:
            dsend[kv, hop] = own.astype(BF16)
            d_copy(kv, hop).start()
        else:
            gk[:, kv * TOKENS : (kv + 1) * TOKENS] = own[:, :TOKENS].astype(BF16)
            gv[:, kv * TOKENS : (kv + 1) * TOKENS] = own[:, TOKENS:].astype(BF16)

    def gating(part):
        g_here = gate[:, part].astype(F32)
        sigma = jax.nn.sigmoid(g_here)
        activation = g_here * sigma
        out_grad = dout[:, part].astype(F32)
        return g_here, sigma, activation, out_grad, out_grad * gain[0:1, part]

    def middle(ch, g):
        part = lanes(ch * CHUNK, CHUNK)
        entered = nn(group(c, g), frecv[1, ch]) * sve[:, part]
        carried[:, part] = entered.astype(BF16)
        here = mixed[:, part] + entered
        mixed[:, part] = here
        _, _, activation, _, scaled = gating(part)
        gated = here * activation
        tsum[0] += folded(gated * gated)
        tsum[1] += folded(gated * scaled)

    def f_leg_b(stage):
        for g in range(groups):
            leg_b(f_copy, fsend, frecv, loc, f_chunk(stage, g), stage)
        for g in range(groups):
            middle(f_chunk(stage, g), g)

    tsum[...] = jnp.zeros_like(tsum)
    dacc[...] = jnp.zeros_like(dacc)
    dgram[...] = jnp.zeros_like(dgram)
    dc[...] = jnp.zeros_like(dc)
    db[...] = jnp.zeros_like(db)
    hsum[...] = jnp.zeros_like(hsum)

    kv_wait(0)
    kv_start(1)
    f_leg_a(1)
    inside_pair(0)
    kv_wait(1)
    kv_start(2)
    f_leg_a(2)
    inside_pair(1)
    kv_wait(2)
    kv_start(3)
    f_leg_a(3)
    f_leg_b(0)
    kv_wait(3)
    for kv in range(KV):
        head = slice(kv * TOKENS, (kv + 1) * TOKENS)
        for slot in range(REACH + 1):
            window = slice(slot * TOKENS, (slot + 1) * TOKENS)
            kall[kv, window] = kw[slot, :, head] if slot < REACH else k[:, head]
            vall[kv, window] = vw[slot, :, head] if slot < REACH else v[:, head]
    attention(0, 0, 2)
    f_leg_b(1)
    attention(0, 2, 4)
    f_leg_b(2)
    d_hop(0, 0)
    attention(1, 0, 2)
    f_leg_b(3)

    ones = jnp.ones((8, TOKENS), F32)
    squares = nt(ones, tsum[0], HIGH)
    crosses = nt(ones, tsum[1], HIGH)
    message = jnp.where(iota((8, TOKENS), 0) == 0, squares, crosses)
    tmsg[...] = message
    tbuf[tp] = message

    def t_copy(peer, slot):
        return remote(tmsg, tbuf.at[slot], tss.at[peer], trs.at[slot], {"tp": peer})

    for peer in tp_peers:
        t_copy(peer, tp).start()
    attention(1, 2, 4)
    d_hop(1, 0)
    d_hop(0, 1)
    for peer in tp_peers:
        t_copy(peer, peer).wait_recv()
    total = tbuf[0] + tbuf[1] + tbuf[2] + tbuf[3]
    factor = lax.rsqrt(total[0:1] / NORM_WIDTH + EPSILON)
    pull = factor * factor * factor * total[1:2] / NORM_WIDTH
    cols[0] = turned(factor)
    cols[1] = turned(pull)

    def cotangents(ch, g):
        part = lanes(ch * CHUNK, CHUNK)
        g_here, sigma, activation, out_grad, scaled = gating(part)
        here = mixed[:, part]
        gated = here * activation
        factor_col = twice(cols[0])
        gated_grad = factor_col * scaled - gated * twice(cols[1])
        mixed_grad = gated_grad * activation
        dy[:, part] = mixed_grad.astype(BF16)
        dsl[ch] = tn(group(c, g), (mixed_grad * sve[:, part]).astype(BF16))
        gate_grad = gated_grad * here * sigma * (1.0 + g_here * (1.0 - sigma))
        ggate[:, part] = gate_grad.astype(BF16)
        rows[2:3, part] = jnp.sum(out_grad * gated * factor_col, axis=0, keepdims=True)

    def side_sums(ch, g):
        part = lanes(ch * CHUNK, CHUNK)
        mixed_grad = dy[:, part].astype(F32)
        mark_part = marks[:, part]
        dc[g] += nt((mixed_grad * sve[:, part]).astype(BF16), frecv[1, ch])
        hsum[0] += nt(mark_part, (mixed_grad * carried[:, part].astype(F32)).astype(BF16))
        hsum[1] += nt(mark_part, (mixed_grad * x[:, part].astype(F32)).astype(BF16))

    for g in range(groups):
        cotangents(b_chunk(0, g), g)
    b_leg_a(0)
    for stage in range(1, 4):
        for g in range(groups):
            cotangents(b_chunk(stage, g), g)

    before = (row_id < lane_id).astype(BF16)
    not_before = row_id >= lane_id

    def inside_back(g, first, last):
        def body(n, _):
            pair = g * pairs + n
            part = lanes(pair * TOKENS, TOKENS)
            dy_part = dy[:, part]
            zero = jnp.zeros_like(dy_part)
            split = jnp.concatenate(
                [jnp.where(left_half, dy_part, zero), jnp.where(left_half, zero, dy_part)], axis=0
            )
            weight_grad = nt(split, x[:, part])
            w_two = w[pl.ds(pair * 2, 2)].reshape(2 * TOKENS, TOKENS)
            ls_two = ls[pl.ds(pair * 2, 2)].reshape(2 * TOKENS, TOKENS)
            spread = weight_grad * ls_two.astype(F32)
            dgram[g] += spread[:TOKENS] + spread[TOKENS:]
            moment = weight_grad * w_two.astype(F32)
            crossing = nn(moment.astype(BF16), before)
            for e in range(2):
                half = slice(e * TOKENS, (e + 1) * TOKENS)
                row = pl.ds(pair * 2 + e, 1)
                heads[3, row, :] = jnp.sum(moment[half], axis=0, keepdims=True)
                heads[4, row, :] = jnp.sum(
                    jnp.where(not_before, crossing[half], 0.0), axis=0, keepdims=True
                )
            dxin[:, part] = tn(w_two, split)
            return 0

        lax.fori_loop(first, last, body, 0)

    def finish(ch, g):
        part = lanes(ch * CHUNK, CHUNK)
        later = brecv[1, ch]
        mark_part = marks[:, part]
        x_part = x[:, part].astype(F32)
        tail_part = tse[:, part]
        scaled_grad = nn(group(b, g), later)
        input_grad = (
            dxin[:, part] + rows[1:2, part] * dy[:, part].astype(F32) + scaled_grad * tail_part
        )
        gx[:, part] = input_grad.astype(BF16)
        hsum[2] += nt(mark_part, (x_part * scaled_grad).astype(BF16))
        hsum[3] += nt(mark_part, (later.astype(F32) * frecv[1, ch].astype(F32)).astype(BF16))
        db[g] += nt((x_part * tail_part).astype(BF16), later)

    def b_leg_b(stage):
        for g in range(groups):
            leg_b(b_copy, bsend, brecv, dsl, b_chunk(stage, g), stage)
        for g in range(groups):
            finish(b_chunk(stage, g), g)

    d_hop(1, 1)
    b_leg_a(1)
    inside_back(0, 0, pairs)
    d_hop(0, 2)
    d_hop(1, 2)
    b_leg_a(2)
    inside_back(1, 0, pairs)
    d_hop(0, 3)
    d_hop(1, 3)
    b_leg_a(3)
    for stage in range(2):
        for g in range(groups):
            side_sums(b_chunk(stage, g), g)
    b_leg_b(0)
    for stage in range(2, 4):
        for g in range(groups):
            side_sums(b_chunk(stage, g), g)
    d_hop(0, 4)
    d_hop(1, 4)
    b_leg_b(1)
    b_leg_b(2)
    b_leg_b(3)

    step = heads[0]
    tail = heads[2]
    rate = jnp.exp(column(rate_log[...]))
    tail_sum = hsum[2]
    over = jnp.sum(hsum[3], axis=1, keepdims=True)
    cum_end = heads[1][:, TOKENS - 1 :]
    whole = jnp.where(begin_last < 0, jnp.exp(cum_end), 0.0)
    log_grad = (
        nn(hsum[0], not_before.astype(F32), HIGH)
        + nn(tail * step * tail_sum, before.astype(F32), HIGH)
        + heads[4]
        + whole * over
    )
    rate_part = -log_grad * rate * step
    pad = jnp.zeros((TOKENS - 2 * n_heads, TOKENS), F32)
    head_sums = nt(ones, jnp.concatenate([hsum[1], rate_part, pad], axis=0), HIGH)
    pieces = channels // TOKENS

    for n in range(pieces):
        zmsg[n : n + 1] = rows[2:3, n * TOKENS : (n + 1) * TOKENS]
    zmsg[pieces : pieces + 8] = head_sums
    zbuf[z] = zmsg[...]

    def z_copy(n, slot):
        return remote(zmsg, zbuf.at[slot], zss.at[n], zrs.at[slot], {"ctx": z_peers[n]})

    for n in range(Z_SIZE - 1):
        z_copy(n, z).start()

    step_grad = heads[3] / step + tail * tail_sum - rate * log_grad
    shifted = raw[...] + column(bias[...])
    graw[...] = jax.nn.sigmoid(shifted) * step_grad
    for g in range(groups):
        spread = dgram[g].astype(BF16)
        part = slice(g * TOKENS, (g + 1) * TOKENS)
        gc[:, part] = (dc[g] + nn(spread, group(b, g))).astype(BF16)
        gb[:, part] = (db[g] + tn(spread, group(c, g))).astype(BF16)

    for n in range(Z_SIZE - 1):
        z_copy(n, lax.rem(z + n + 1, Z_SIZE)).wait_recv()
    total = zbuf[0]
    for n in range(1, Z_SIZE):
        total = total + zbuf[n]
    xmsg[...] = total
    xbuf[xc] = total

    def x_copy(n, slot):
        return remote(xmsg, xbuf.at[slot], xss.at[n], xrs.at[slot], xc_ids[n])

    for n in range(X_SIZE * CORES - 1):
        x_copy(n, xc).start()
    for n in range(X_SIZE * CORES - 1):
        x_copy(n, xc_peers[n]).wait_recv()
    total = xbuf[0]
    for n in range(1, X_SIZE * CORES):
        total = total + xbuf[n]
    for n in range(pieces):
        ggain[0:1, n * TOKENS : (n + 1) * TOKENS] = total[n : n + 1]
    gskip[...] = total[pieces : pieces + 1, :n_heads]
    grate[...] = total[pieces : pieces + 1, n_heads : 2 * n_heads]

    for hop in range(REACH):
        for copy in kv_copies(hop):
            copy.wait_send()
        for kv in range(KV):
            d_copy(kv, hop).wait_send()
    for copy, chunk in ((f_copy, f_chunk), (b_copy, b_chunk)):
        for stage in range(4):
            for g in range(groups):
                ch = chunk(stage, g)
                copy(0, ch, 0).wait_send()
                if stage < 3:
                    copy(1, ch, 1).wait_send()
    for peer in tp_peers:
        t_copy(peer, tp).wait_send()
    for n in range(Z_SIZE - 1):
        z_copy(n, z).wait_send()
    for n in range(X_SIZE * CORES - 1):
        x_copy(n, xc).wait_send()


def per_device(
    ssm_input, ssm_gate, step_raw, b_proj, c_proj, rate_log, step_bias, skip_gain, norm_gain,
    ssm_grad_out, queries, keys, values, attention_output_gradient, doc_lengths,
):
    channels = ssm_input.shape[2]
    n_heads = rate_log.shape[0]
    groups = b_proj.shape[2] // TOKENS
    chunks = channels // CHUNK
    vmem = pl.BlockSpec(memory_space=pltpu.VMEM)
    smem = pl.BlockSpec(memory_space=pltpu.SMEM)
    wide = jax.ShapeDtypeStruct((TOKENS, channels), BF16)
    narrow = jax.ShapeDtypeStruct((TOKENS, groups * TOKENS), BF16)
    head_row = jax.ShapeDtypeStruct((1, n_heads), F32)
    square = (TOKENS, TOKENS)
    chunked = (chunks, TOKENS, CHUNK)
    window = (REACH + 1) * TOKENS
    message = (channels // TOKENS + 8, TOKENS)
    dma = pltpu.SemaphoreType.DMA
    scratch = [
        pltpu.VMEM((n_heads,) + square, BF16),
        pltpu.VMEM((n_heads,) + square, BF16),
        pltpu.VMEM((TOKENS, channels), F32),
        pltpu.VMEM((TOKENS, channels), BF16),
        pltpu.VMEM((TOKENS, channels), BF16),
        pltpu.VMEM((TOKENS, channels), F32),
        pltpu.VMEM((TOKENS, channels), F32),
        pltpu.VMEM((TOKENS, channels), F32),
        pltpu.VMEM((8, channels), F32),
        pltpu.VMEM((n_heads, channels), BF16),
        pltpu.VMEM((5, n_heads, TOKENS), F32),
        pltpu.VMEM((groups,) + square, F32),
        pltpu.VMEM((groups,) + square, F32),
        pltpu.VMEM(chunked, F32),
        pltpu.VMEM(chunked, F32),
        pltpu.VMEM((2,) + chunked, BF16),
        pltpu.VMEM((2,) + chunked, BF16),
        pltpu.VMEM((2,) + chunked, BF16),
        pltpu.VMEM((2,) + chunked, BF16),
        pltpu.VMEM((REACH, TOKENS, KV * TOKENS), BF16),
        pltpu.VMEM((REACH, TOKENS, KV * TOKENS), BF16),
        pltpu.VMEM((KV, window, TOKENS), BF16),
        pltpu.VMEM((KV, window, TOKENS), BF16),
        pltpu.VMEM((KV, window, 2 * TOKENS), F32),
        pltpu.VMEM((KV, REACH, TOKENS, 2 * TOKENS), BF16),
        pltpu.VMEM((KV, REACH, TOKENS, 2 * TOKENS), BF16),
        pltpu.VMEM((2,) + square, F32),
        pltpu.VMEM((8, TOKENS), F32),
        pltpu.VMEM((TP_SIZE, 8, TOKENS), F32),
        pltpu.VMEM((2,) + square, F32),
        pltpu.VMEM((groups,) + square, F32),
        pltpu.VMEM((groups,) + square, F32),
        pltpu.VMEM((4, n_heads, TOKENS), F32),
        pltpu.VMEM(message, F32),
        pltpu.VMEM((Z_SIZE,) + message, F32),
        pltpu.VMEM(message, F32),
        pltpu.VMEM((X_SIZE * CORES,) + message, F32),
        dma((2, chunks)),
        dma((2, chunks)),
        dma((2, chunks)),
        dma((2, chunks)),
        dma((2, REACH)),
        dma((2, REACH)),
        dma((KV, REACH)),
        dma((KV, REACH)),
        dma((TP_SIZE,)),
        dma((TP_SIZE,)),
        dma((Z_SIZE,)),
        dma((Z_SIZE,)),
        dma((X_SIZE * CORES,)),
        dma((X_SIZE * CORES,)),
    ]
    results = pl.pallas_call(
        kernel,
        out_shape=(
            wide,
            wide,
            jax.ShapeDtypeStruct((n_heads, TOKENS), F32),
            narrow,
            narrow,
            head_row,
            head_row,
            jax.ShapeDtypeStruct((1, channels), F32),
            wide,
            narrow,
            narrow,
        ),
        in_specs=[smem] + [vmem] * 14,
        out_specs=(vmem,) * 11,
        scratch_shapes=scratch,
        compiler_params=pltpu.CompilerParams(
            collective_id=0, has_side_effects=True, vmem_limit_bytes=60 * 1024 * 1024
        ),
        name="mixer_and_attention",
    )(
        doc_lengths,
        ssm_input[0],
        ssm_gate[0],
        step_raw[0],
        b_proj[0],
        c_proj[0],
        rate_log[None],
        step_bias[None],
        skip_gain[None],
        norm_gain[None],
        ssm_grad_out[0],
        queries[0],
        keys[0],
        values[0],
        attention_output_gradient[0],
    )
    gx, ggate, graw, gb, gc, grate, gskip, ggain, gq, gk, gv = results
    return (
        gx[None], ggate[None], graw[None], gb[None], gc[None],
        grate[0], gskip[0], ggain[0], gq[None], gk[None], gv[None],
    )


def solution(mesh):
    tokens = P("dp", "ctx", "tp")
    steps = P("dp", "tp", "ctx")
    param = P("tp")
    return jax.shard_map(
        per_device,
        mesh=mesh,
        in_specs=(
            tokens, tokens, steps, tokens, tokens, param, param, param, param,
            tokens, tokens, tokens, tokens, tokens, P("dp", None),
        ),
        out_specs=(
            tokens, tokens, steps, tokens, tokens, param, param, param,
            tokens, tokens, tokens,
        ),
        check_vma=False,
    )
```

time: 788 us -> 109 us (0.14); the launches traced: 779 us -> 109 us
  waiting for transfers between devices: 347 us -> 0 us
  blocking collectives: 202 us -> 0 us
  Pallas kernels: 0 us -> 99.2 us
  other arithmetic: 70.7 us -> 0 us
  local copies, waits for them, and re-layouts: 72.8 us -> 8.99 us
  matrix products: 31.7 us -> 0 us
  starting transfers between devices: 24.2 us -> 0 us
  between operations: 18.5 us -> 0.68 us
  loops' own time: 11.9 us -> 0 us
    all_gather x2 -> x0, waiting for transfers between devices: 314 us -> none  [carried_in_2(): gathered = jax.tree.map(lambda a: lax.all_gather(a, axis), part)]
    psum x2 -> x0, blocking collectives: 137 us -> none  [the longest x1 129 us: per_device(): lax.psum((rate_grad, local_grads[6], gain_grad), ('ctx', 'dp'))]
    pallas_call x0 -> x1, Pallas kernels: none -> 99.2 us  [per_device(): pl.pallas_call(kernel, out_shape=(wide, wide, jax.ShapeDtypeStruct((n_hea...]
    unnamed x1 -> x0, blocking collectives: 65.1 us -> none
    add x38 -> x0, other arithmetic: 45.3 us -> none  [the longest x31 44.6 us: chain_step(): later[0][:, None, None] * earlier[1] + later[1]]
    ppermute x8 -> x0, waiting for transfers between devices: 32.7 us -> none  [passed_along(): return lax.ppermute(shard, axis, pairs)]
    dot_general x21 -> x0, matrix products: 31.7 us -> none  [the longest x3 11.2 us: advance(): inside = jnp.einsum('gjts,sgjp->tgjp', weights, x_here, precision=precise)]
    ppermute x8 -> x0, starting transfers between devices: 24.1 us -> none  [passed_along(): return lax.ppermute(shard, axis, pairs)]
  transfers between devices with their start and end apart: 10 -> 0, of which waited for: 9 -> 0; matrix products, arithmetic and copies ran while one was open for 9% -> 0% of each run, Pallas kernels for 0% -> 0%
where the time goes in v1:
time: 109 us
  Pallas kernels  99.2 us (91%)
  local copies, waits for them, and re-layouts  8.99 us (8%)
    pallas_call x1, Pallas kernels, per_device(): pl.pallas_call(kernel, out_shape=(wide, wide, jax.ShapeDtypeStruct((n_hea...  99.2 us
    unnamed x31, local copies, waits for them, and re-layouts  8.99 us

profile of v1, /device:TPU:1, one launch (start us, length us, event | category | flops | bytes accessed | tf_op | source)
XLA Modules:
  0.0 108.9 jit_solution(7957969733461565054)
XLA Ops:
  0.6 99.2 %mixer_and_attention.1 = (bf16[128,2048]{1,0:T(8,128)(2,1)}, bf16[128,2048]{1,0:T(8,128)(2,1)}, f32[32,128]{1,0:T(8,128)}, bf16[128,256]{1,0:T(8,128)(2,1)}, bf1...) custom-call(s32[1,17]{1,0:T(1,128)} %lens.1, ...), custom_call_target="tpu_custom_call" | custom-call | tf_op jit(solution)/shard_map/mixer_and_attention/pallas_call | solution.py:641
  99.8 0.0 copy-start.1
  99.8 1.9 %copy.37 = bf16[1,128,2048]{2,1,0:T(8,128)(2,1)} copy(bf16[1,128,2048]{2,1,0:T(8,128)(2,1)} %bitcast.32) | data formatting | bytes 1048576
  101.8 0.0 copy-done.1
  101.8 0.0 copy-start.6
  101.8 0.0 copy-start.5
  101.8 0.0 copy-start
  101.8 0.8 copy.38
  102.6 0.0 copy-done.6
  102.6 0.6 copy.39
  103.2 0.0 copy-done.5
  103.2 0.0 copy-start.4
  103.2 0.6 copy.40
  103.8 0.2 copy-done.4
  104.1 0.0 copy-start.9
  104.1 0.0 copy-start.7
  104.1 0.6 copy.41
  104.7 0.0 copy-done.9
  104.7 0.0 copy-start.8
  104.7 0.5 copy.42
  105.2 0.2 copy-done.8
  105.4 0.5 copy.43
  105.9 0.0 copy-done.7
  105.9 0.6 copy.44
  106.5 0.0 copy-done
  106.5 0.0 copy-start.3
  106.5 0.8 copy.45
  107.3 0.1 copy-done.3
  107.4 0.0 copy-start.2
  107.4 0.6 copy.46
  108.0 0.2 copy-done.2
  108.2 0.6 copy.47
Async XLA Ops:
  99.8 2.0 %copy-start.1 = (bf16[128,2048]{1,0:T(8,128)(2,1)S(1)}, bf16[128,2048]{1,0:T(8,128)(2,1)}, u32[]{:S(2)}) copy-start(bf16[128,2048]{1,0:T(8,128)(2,1)} %get-tuple-element.23) | copy-start | bytes 1572868
  101.8 0.8 copy-start.6
  101.8 1.4 %copy-start.5 = (bf16[128,256]{1,0:T(8,128)(2,1)S(1)}, bf16[128,256]{1,0:T(8,128)(2,1)}, u32[]{:S(2)}) copy-start(bf16[128,256]{1,0:T(8,128)(2,1)} %get-tuple-element.25) | copy-start | bytes 196612
  101.8 4.7 %copy-start = (bf16[128,2048]{1,0:T(8,128)(2,1)S(1)}, bf16[128,2048]{1,0:T(8,128)(2,1)}, u32[]{:S(2)}) copy-start(bf16[128,2048]{1,0:T(8,128)(2,1)} %get-tuple-element.30) | copy-start | bytes 1572868
  103.2 0.9 copy-start.4
  104.1 0.6 copy-start.9
  104.1 1.8 %copy-start.7 = (f32[1,2048]{1,0:T(1,128)S(1)}, f32[1,2048]{1,0:T(1,128)}, u32[]{:S(2)}) copy-start(f32[1,2048]{1,0:T(1,128)} %get-tuple-element.29) | copy-start | bytes 24580
  104.7 0.7 copy-start.8
  106.5 0.9 copy-start.3
  107.4 0.9 copy-start.2

commit v2 on v1

--- a/solution.py
+++ b/solution.py
@@ -14,6 +14,7 @@
 WIDE = 64
 REACH = 4
 CHUNK = 256
+CUT = 64
 KV = 2
 NORM_WIDTH = 8192
 EPSILON = 1e-05
@@ -22,6 +23,7 @@
 Z_SIZE = 8
 X_SIZE = 4
 CORES = 2
+VMEM_LIMIT = 62000000
 TP_SIZE = 4
 
 
@@ -70,12 +72,14 @@
 
 
 def kernel(
-    lens, x, gate, raw, b, c, rate_log, bias, skip, gain, dout, q, k, v, do,
+    lens, x_in, gate_in, raw_in, b_in, c_in, rate_log, bias, skip, gain,
+    dout_in, q_in, k_in, v_in, do_in,
     gx, ggate, graw, gb, gc, grate, gskip, ggain, gq, gk, gv,
     ls, w, mixed, carried, dy, dxin, sve, tse, rows, marks, heads,
     gram, dgram, loc, dsl, fsend, frecv, bsend, brecv, kw, vw, kall, vall,
     dacc, dsend, drecv, tsum, tmsg, tbuf, cols, dc, db, hsum, zmsg, zbuf, xmsg, xbuf,
-    fss, frs, bss, brs, kss, krs, dss, drs, tss, trs, zss, zrs, xss, xrs,
+    zlate, zlbuf, xlate, xlbuf, x, gate, raw, b, c, dout, q, k, v, do,
+    fss, frs, bss, brs, kss, krs, dss, drs, tss, trs, zss, zrs, xss, xrs, ins,
 ):
     i = lax.axis_index("ctx")
     core = lax.axis_index("dp")
@@ -104,7 +108,19 @@
     )
     for device in greeted:
         pl.semaphore_signal(barrier, inc=1, device_id=device, device_id_type=MESH)
-    pl.semaphore_wait(barrier, len(greeted))
+
+    loads = []
+    for source, target in (
+        (raw_in, raw), (x_in, x), (b_in, b), (c_in, c), (k_in, k), (v_in, v),
+        (gate_in, gate), (dout_in, dout), (q_in, q), (do_in, do),
+    ):
+        loads.append((target, pltpu.make_async_copy(source, target, ins.at[len(loads)])))
+        loads[-1][1].start()
+
+    def loaded(*targets):
+        for target, load in loads:
+            if any(target is wanted for wanted in targets):
+                load.wait()
 
     def remote(source, target, send, recv, device):
         return pltpu.make_async_remote_copy(
@@ -133,8 +149,6 @@
     def kv_wait(hop):
         for copy in kv_copies(hop):
             copy.wait_recv()
-
-    kv_start(0)
 
     base = i * TOKENS
     position = iota((8, TOKENS), 1) + base
@@ -151,6 +165,7 @@
     within = (lane_id <= row_id) & (lane_id.astype(F32) >= begin_col)
     up_to = (row_id <= lane_id).astype(F32)
 
+    loaded(raw)
     shifted = raw[...] + column(bias[...])
     step = jax.nn.softplus(shifted)
     rate = jnp.exp(column(rate_log[...]))
@@ -190,8 +205,12 @@
         return g * 4 + lax.rem(stage + i, 4)
 
     def chain(send, recv, ss, rs, device):
-        def copy(leg, ch, to):
-            return remote(send.at[leg, ch], recv.at[to, ch], ss.at[leg, ch], rs.at[to, ch], device)
+        def copy(leg, ch, to, n):
+            cut = slice(n * CUT, (n + 1) * CUT)
+            return remote(
+                send.at[leg, ch, cut], recv.at[to, ch, cut],
+                ss.at[leg, ch, n], rs.at[to, ch, n], device,
+            )
 
         return copy
 
@@ -199,19 +218,24 @@
     b_copy = chain(bsend, brecv, bss, brs, {"ctx": left})
 
     def leg_a(copy, send, recv, own, ch, stage):
-        value = own[ch]
-        if stage > 0:
-            copy(0, ch, 0).wait_recv()
-            value = value + rows[0:1, lanes(ch * CHUNK, CHUNK)] * recv[0, ch].astype(F32)
-        send[0, ch] = value.astype(BF16)
-        copy(0, ch, 1 if stage == 3 else 0).start()
+        for n in range(TOKENS // CUT):
+            cut = slice(n * CUT, (n + 1) * CUT)
+            value = own[ch, cut]
+            if stage > 0:
+                copy(0, ch, 0, n).wait_recv()
+                decayed = rows[0:1, lanes(ch * CHUNK, CHUNK)] * recv[0, ch, cut].astype(F32)
+                value = value + decayed
+            send[0, ch, cut] = value.astype(BF16)
+            copy(0, ch, 1 if stage == 3 else 0, n).start()
 
     def leg_b(copy, send, recv, own, ch, stage):
-        copy(1, ch, 1).wait_recv()
-        if stage < 3:
-            value = own[ch] + rows[0:1, lanes(ch * CHUNK, CHUNK)] * recv[1, ch].astype(F32)
-            send[1, ch] = value.astype(BF16)
-            copy(1, ch, 1).start()
+        for n in range(TOKENS // CUT):
+            cut = slice(n * CUT, (n + 1) * CUT)
+            copy(1, ch, 1, n).wait_recv()
+            if stage < 3:
+                decayed = rows[0:1, lanes(ch * CHUNK, CHUNK)] * recv[1, ch, cut].astype(F32)
+                send[1, ch, cut] = (own[ch, cut] + decayed).astype(BF16)
+                copy(1, ch, 1, n).start()
 
     def f_leg_a(stage):
         for g in range(groups):
@@ -221,20 +245,25 @@
         for g in range(groups):
             leg_a(b_copy, bsend, brecv, dsl, b_chunk(stage, g), stage)
 
+    loaded(x, b)
     for g in range(groups):
         local_state(f_chunk(0, g), g)
+    pl.semaphore_wait(barrier, len(greeted))
     f_leg_a(0)
+    loaded(k, v)
+    kv_start(0)
     for stage in range(1, 4):
         for g in range(groups):
             local_state(f_chunk(stage, g), g)
     sve[...] = expand(survive)
     rows[1:2] = jnp.sum(jnp.where(mark, column(skip[...]), 0.0), axis=0, keepdims=True)
+    loaded(c)
     for g in range(groups):
         gram[g] = nt(group(c, g), group(b, g))
 
     left_half = iota((1, TOKENS), 1) < WIDE
 
-    def inside_pair(g):
+    def inside_pair(g, first, last):
         def body(n, _):
             pair = g * pairs + n
             part = lanes(pair * TOKENS, TOKENS)
@@ -251,7 +280,7 @@
             mixed[:, part] = inside + rows[1:2, part] * x_part.astype(F32)
             return 0
 
-        lax.fori_loop(0, pairs, body, 0)
+        lax.fori_loop(first, last, body, 0)
 
     def attention(kv, first, last):
         key = kall[kv]
@@ -322,6 +351,8 @@
     def f_leg_b(stage):
         for g in range(groups):
             leg_b(f_copy, fsend, frecv, loc, f_chunk(stage, g), stage)
+
+    def f_middle(stage):
         for g in range(groups):
             middle(f_chunk(stage, g), g)
 
@@ -332,32 +363,32 @@
     db[...] = jnp.zeros_like(db)
     hsum[...] = jnp.zeros_like(hsum)
 
+    def gather_window():
+        for kv in range(KV):
+            head = slice(kv * TOKENS, (kv + 1) * TOKENS)
+            for slot in range(REACH + 1):
+                window = slice(slot * TOKENS, (slot + 1) * TOKENS)
+                kall[kv, window] = kw[slot, :, head] if slot < REACH else k[:, head]
+                vall[kv, window] = vw[slot, :, head] if slot < REACH else v[:, head]
+
+    f_leg_a(1)
+    inside_pair(0, 0, 8)
+    f_leg_a(2)
+    inside_pair(1, 0, 8)
+    f_leg_a(3)
     kv_wait(0)
     kv_start(1)
-    f_leg_a(1)
-    inside_pair(0)
+    loaded(gate, dout, q, do)
+    f_leg_b(0)
+    f_middle(0)
+    f_leg_b(1)
+    f_middle(1)
+    f_leg_b(2)
+    f_middle(2)
+    f_leg_b(3)
     kv_wait(1)
     kv_start(2)
-    f_leg_a(2)
-    inside_pair(1)
-    kv_wait(2)
-    kv_start(3)
-    f_leg_a(3)
-    f_leg_b(0)
-    kv_wait(3)
-    for kv in range(KV):
-        head = slice(kv * TOKENS, (kv + 1) * TOKENS)
-        for slot in range(REACH + 1):
-            window = slice(slot * TOKENS, (slot + 1) * TOKENS)
-            kall[kv, window] = kw[slot, :, head] if slot < REACH else k[:, head]
-            vall[kv, window] = vw[slot, :, head] if slot < REACH else v[:, head]
-    attention(0, 0, 2)
-    f_leg_b(1)
-    attention(0, 2, 4)
-    f_leg_b(2)
-    d_hop(0, 0)
-    attention(1, 0, 2)
-    f_leg_b(3)
+    f_middle(3)
 
     ones = jnp.ones((8, TOKENS), F32)
     squares = nt(ones, tsum[0], HIGH)
@@ -371,9 +402,6 @@
 
     for peer in tp_peers:
         t_copy(peer, tp).start()
-    attention(1, 2, 4)
-    d_hop(1, 0)
-    d_hop(0, 1)
     for peer in tp_peers:
         t_copy(peer, peer).wait_recv()
     total = tbuf[0] + tbuf[1] + tbuf[2] + tbuf[3]
@@ -442,49 +470,108 @@
 
         lax.fori_loop(first, last, body, 0)
 
-    def finish(ch, g):
+    def tail_rates(ch, g):
         part = lanes(ch * CHUNK, CHUNK)
         later = brecv[1, ch]
         mark_part = marks[:, part]
-        x_part = x[:, part].astype(F32)
-        tail_part = tse[:, part]
         scaled_grad = nn(group(b, g), later)
-        input_grad = (
-            dxin[:, part] + rows[1:2, part] * dy[:, part].astype(F32) + scaled_grad * tail_part
-        )
-        gx[:, part] = input_grad.astype(BF16)
-        hsum[2] += nt(mark_part, (x_part * scaled_grad).astype(BF16))
+        hsum[2] += nt(mark_part, (x[:, part].astype(F32) * scaled_grad).astype(BF16))
         hsum[3] += nt(mark_part, (later.astype(F32) * frecv[1, ch].astype(F32)).astype(BF16))
-        db[g] += nt((x_part * tail_part).astype(BF16), later)
+        dxin[:, part] += rows[1:2, part] * dy[:, part].astype(F32) + scaled_grad * tse[:, part]
+
+    def finish(ch, g):
+        part = lanes(ch * CHUNK, CHUNK)
+        gx[:, part] = dxin[:, part].astype(BF16)
+        db[g] += nt((x[:, part].astype(F32) * tse[:, part]).astype(BF16), brecv[1, ch])
 
     def b_leg_b(stage):
         for g in range(groups):
             leg_b(b_copy, bsend, brecv, dsl, b_chunk(stage, g), stage)
+
+    def at_stage(work, stage):
         for g in range(groups):
-            finish(b_chunk(stage, g), g)
-
+            work(b_chunk(stage, g), g)
+
+    pieces = channels // TOKENS
+    z_refs = ((zmsg, zbuf), (zlate, zlbuf))
+    x_refs = ((xmsg, xbuf), (xlate, xlbuf))
+
+    def padded(a):
+        return jnp.concatenate([a, jnp.zeros((TOKENS - a.shape[0], TOKENS), F32)], axis=0)
+
+    def z_copy(turn, n, slot):
+        message, slots = z_refs[turn]
+        return remote(
+            message, slots.at[slot], zss.at[turn, n], zrs.at[turn, slot], {"ctx": z_peers[n]}
+        )
+
+    def x_copy(turn, n, slot):
+        message, slots = x_refs[turn]
+        return remote(message, slots.at[slot], xss.at[turn, n], xrs.at[turn, slot], xc_ids[n])
+
+    def z_start(turn):
+        message, slots = z_refs[turn]
+        slots[z] = message[...]
+        for n in range(Z_SIZE - 1):
+            z_copy(turn, n, z).start()
+
+    def x_start(turn):
+        slots = z_refs[turn][1]
+        for n in range(Z_SIZE - 1):
+            z_copy(turn, n, lax.rem(z + n + 1, Z_SIZE)).wait_recv()
+        total = slots[0]
+        for n in range(1, Z_SIZE):
+            total = total + slots[n]
+        message, slots = x_refs[turn]
+        message[...] = total
+        slots[xc] = total
+        for n in range(X_SIZE * CORES - 1):
+            x_copy(turn, n, xc).start()
+
+    def x_total(turn):
+        slots = x_refs[turn][1]
+        for n in range(X_SIZE * CORES - 1):
+            x_copy(turn, n, xc_peers[n]).wait_recv()
+        total = slots[0]
+        for n in range(1, X_SIZE * CORES):
+            total = total + slots[n]
+        return total
+
+    def early_sums():
+        for n in range(pieces):
+            zmsg[n : n + 1] = rows[2:3, n * TOKENS : (n + 1) * TOKENS]
+        zmsg[pieces : pieces + 8] = nt(ones, padded(hsum[1]), HIGH)
+        z_start(0)
+
+    kv_wait(2)
+    kv_start(3)
+    inside_back(0, 0, pairs)
+    b_leg_a(1)
+    kv_wait(3)
+    gather_window()
+    attention(0, 0, 2)
+    b_leg_a(2)
+    attention(0, 2, 4)
+    b_leg_a(3)
+    d_hop(0, 0)
+    attention(1, 0, 2)
+    b_leg_b(0)
+    d_hop(0, 1)
+    attention(1, 2, 4)
+    b_leg_b(1)
+    d_hop(1, 0)
+    inside_back(1, 0, pairs)
+    d_hop(0, 2)
+    b_leg_b(2)
+    for stage in range(3):
+        at_stage(tail_rates, stage)
+    for stage in range(4):
+        at_stage(side_sums, stage)
+    early_sums()
     d_hop(1, 1)
-    b_leg_a(1)
-    inside_back(0, 0, pairs)
-    d_hop(0, 2)
-    d_hop(1, 2)
-    b_leg_a(2)
-    inside_back(1, 0, pairs)
     d_hop(0, 3)
-    d_hop(1, 3)
-    b_leg_a(3)
-    for stage in range(2):
-        for g in range(groups):
-            side_sums(b_chunk(stage, g), g)
-    b_leg_b(0)
-    for stage in range(2, 4):
-        for g in range(groups):
-            side_sums(b_chunk(stage, g), g)
-    d_hop(0, 4)
-    d_hop(1, 4)
-    b_leg_b(1)
-    b_leg_b(2)
     b_leg_b(3)
+    at_stage(tail_rates, 3)
 
     step = heads[0]
     tail = heads[2]
@@ -500,20 +587,14 @@
         + whole * over
     )
     rate_part = -log_grad * rate * step
-    pad = jnp.zeros((TOKENS - 2 * n_heads, TOKENS), F32)
-    head_sums = nt(ones, jnp.concatenate([hsum[1], rate_part, pad], axis=0), HIGH)
-    pieces = channels // TOKENS
-
-    for n in range(pieces):
-        zmsg[n : n + 1] = rows[2:3, n * TOKENS : (n + 1) * TOKENS]
-    zmsg[pieces : pieces + 8] = head_sums
-    zbuf[z] = zmsg[...]
-
-    def z_copy(n, slot):
-        return remote(zmsg, zbuf.at[slot], zss.at[n], zrs.at[slot], {"ctx": z_peers[n]})
-
-    for n in range(Z_SIZE - 1):
-        z_copy(n, z).start()
+    zlate[...] = nt(ones, padded(rate_part), HIGH)
+    z_start(1)
+    d_hop(1, 2)
+    for stage in range(4):
+        at_stage(finish, stage)
+    d_hop(0, 4)
+    x_start(0)
+    d_hop(1, 3)
 
     step_grad = heads[3] / step + tail * tail_sum - rate * log_grad
     shifted = raw[...] + column(bias[...])
@@ -524,28 +605,14 @@
         gc[:, part] = (dc[g] + nn(spread, group(b, g))).astype(BF16)
         gb[:, part] = (db[g] + tn(spread, group(c, g))).astype(BF16)
 
-    for n in range(Z_SIZE - 1):
-        z_copy(n, lax.rem(z + n + 1, Z_SIZE)).wait_recv()
-    total = zbuf[0]
-    for n in range(1, Z_SIZE):
-        total = total + zbuf[n]
-    xmsg[...] = total
-    xbuf[xc] = total
-
-    def x_copy(n, slot):
-        return remote(xmsg, xbuf.at[slot], xss.at[n], xrs.at[slot], xc_ids[n])
-
-    for n in range(X_SIZE * CORES - 1):
-        x_copy(n, xc).start()
-    for n in range(X_SIZE * CORES - 1):
-        x_copy(n, xc_peers[n]).wait_recv()
-    total = xbuf[0]
-    for n in range(1, X_SIZE * CORES):
-        total = total + xbuf[n]
+    x_start(1)
+    d_hop(1, 4)
+    total = x_total(0)
     for n in range(pieces):
         ggain[0:1, n * TOKENS : (n + 1) * TOKENS] = total[n : n + 1]
     gskip[...] = total[pieces : pieces + 1, :n_heads]
-    grate[...] = total[pieces : pieces + 1, n_heads : 2 * n_heads]
+    total = x_total(1)
+    grate[...] = total[0:1, :n_heads]
 
     for hop in range(REACH):
         for copy in kv_copies(hop):
@@ -556,15 +623,29 @@
         for stage in range(4):
             for g in range(groups):
                 ch = chunk(stage, g)
-                copy(0, ch, 0).wait_send()
-                if stage < 3:
-                    copy(1, ch, 1).wait_send()
+                for n in range(TOKENS // CUT):
+                    copy(0, ch, 0, n).wait_send()
+                    if stage < 3:
+                        copy(1, ch, 1, n).wait_send()
     for peer in tp_peers:
         t_copy(peer, tp).wait_send()
-    for n in range(Z_SIZE - 1):
-        z_copy(n, z).wait_send()
-    for n in range(X_SIZE * CORES - 1):
-        x_copy(n, xc).wait_send()
+    for turn in range(2):
+        for n in range(Z_SIZE - 1):
+            z_copy(turn, n, z).wait_send()
+        for n in range(X_SIZE * CORES - 1):
+            x_copy(turn, n, xc).wait_send()
+
+
+def hand_over(*refs):
+    results, outputs, sems = refs[:11], refs[11:22], refs[22]
+    copies = [
+        pltpu.make_async_copy(result, output, sems.at[n])
+        for n, (result, output) in enumerate(zip(results, outputs))
+    ]
+    for copy in copies:
+        copy.start()
+    for copy in copies:
+        copy.wait()
 
 
 def per_device(
@@ -576,6 +657,8 @@
     groups = b_proj.shape[2] // TOKENS
     chunks = channels // CHUNK
     vmem = pl.BlockSpec(memory_space=pltpu.VMEM)
+    hbm = pl.BlockSpec(memory_space=pltpu.HBM)
+    anywhere = pl.BlockSpec(memory_space=pl.ANY)
     smem = pl.BlockSpec(memory_space=pltpu.SMEM)
     wide = jax.ShapeDtypeStruct((TOKENS, channels), BF16)
     narrow = jax.ShapeDtypeStruct((TOKENS, groups * TOKENS), BF16)
@@ -623,41 +706,48 @@
         pltpu.VMEM((Z_SIZE,) + message, F32),
         pltpu.VMEM(message, F32),
         pltpu.VMEM((X_SIZE * CORES,) + message, F32),
-        dma((2, chunks)),
-        dma((2, chunks)),
-        dma((2, chunks)),
-        dma((2, chunks)),
+        pltpu.VMEM((8, TOKENS), F32),
+        pltpu.VMEM((Z_SIZE, 8, TOKENS), F32),
+        pltpu.VMEM((8, TOKENS), F32),
+        pltpu.VMEM((X_SIZE * CORES, 8, TOKENS), F32),
+        pltpu.VMEM(wide.shape, BF16),
+        pltpu.VMEM(wide.shape, BF16),
+        pltpu.VMEM((n_heads, TOKENS), F32),
+        pltpu.VMEM(narrow.shape, BF16),
+        pltpu.VMEM(narrow.shape, BF16),
+        pltpu.VMEM(wide.shape, BF16),
+        pltpu.VMEM(wide.shape, BF16),
+        pltpu.VMEM(narrow.shape, BF16),
+        pltpu.VMEM(narrow.shape, BF16),
+        pltpu.VMEM(wide.shape, BF16),
+        dma((2, chunks, TOKENS // CUT)),
+        dma((2, chunks, TOKENS // CUT)),
+        dma((2, chunks, TOKENS // CUT)),
+        dma((2, chunks, TOKENS // CUT)),
         dma((2, REACH)),
         dma((2, REACH)),
         dma((KV, REACH)),
         dma((KV, REACH)),
         dma((TP_SIZE,)),
         dma((TP_SIZE,)),
-        dma((Z_SIZE,)),
-        dma((Z_SIZE,)),
-        dma((X_SIZE * CORES,)),
-        dma((X_SIZE * CORES,)),
+        dma((2, Z_SIZE)),
+        dma((2, Z_SIZE)),
+        dma((2, X_SIZE * CORES)),
+        dma((2, X_SIZE * CORES)),
+        dma((10,)),
     ]
+    shapes = (
+        wide, wide, jax.ShapeDtypeStruct((n_heads, TOKENS), F32), narrow, narrow, head_row,
+        head_row, jax.ShapeDtypeStruct((1, channels), F32), wide, narrow, narrow,
+    )
     results = pl.pallas_call(
         kernel,
-        out_shape=(
-            wide,
-            wide,
-            jax.ShapeDtypeStruct((n_heads, TOKENS), F32),
-            narrow,
-            narrow,
-            head_row,
-            head_row,
-            jax.ShapeDtypeStruct((1, channels), F32),
-            wide,
-            narrow,
-            narrow,
-        ),
-        in_specs=[smem] + [vmem] * 14,
+        out_shape=shapes,
+        in_specs=[smem] + [hbm] * 5 + [vmem] * 4 + [hbm] * 5,
         out_specs=(vmem,) * 11,
         scratch_shapes=scratch,
         compiler_params=pltpu.CompilerParams(
-            collective_id=0, has_side_effects=True, vmem_limit_bytes=60 * 1024 * 1024
+            collective_id=0, has_side_effects=True, vmem_limit_bytes=VMEM_LIMIT
         ),
         name="mixer_and_attention",
     )(
@@ -677,6 +767,15 @@
         values[0],
         attention_output_gradient[0],
     )
+    results = pl.pallas_call(
+        hand_over,
+        out_shape=shapes,
+        in_specs=[vmem] * 11,
+        out_specs=(anywhere,) * 11,
+        scratch_shapes=[dma((11,))],
+        compiler_params=pltpu.CompilerParams(vmem_limit_bytes=VMEM_LIMIT),
+        name="hand_over",
+    )(*results)
     gx, ggate, graw, gb, gc, grate, gskip, ggain, gq, gk, gv = results
     return (
         gx[None], ggate[None], graw[None], gb[None], gc[None],

time: 109 us -> 95 us (0.87)
  local copies, waits for them, and re-layouts: 8.99 us -> 0 us
  Pallas kernels: 99.2 us -> 94.1 us
    unnamed x31 -> x0, local copies, waits for them, and re-layouts: 8.99 us -> none
    pallas_call x1 -> x2, Pallas kernels: 99.2 us -> 94.1 us  [the longest x1 91.3 us: per_device(): pl.pallas_call(kernel, out_shape=shapes, in_specs=[smem] + [hbm] * 5 + [v...]
where the time goes in v2:
time: 95 us; the launch traced here: 94.8 us
  Pallas kernels  94.1 us (99%)
    pallas_call x1, Pallas kernels, per_device(): pl.pallas_call(kernel, out_shape=shapes, in_specs=[smem] + [hbm] * 5 + [v...  91.3 us
    pallas_call x1, Pallas kernels, per_device(): pl.pallas_call(hand_over, out_shape=shapes, in_specs=[vmem] * 11, out_spe...  2.8 us

profile of v2, /device:TPU:1, one launch (start us, length us, event | category | flops | bytes accessed | tf_op | source)
XLA Modules:
  0.0 94.8 jit_solution(17279268472584790176)
XLA Ops:
  0.6 91.3 %mixer_and_attention.1 = (bf16[128,2048]{1,0:T(8,128)(2,1)}, bf16[128,2048]{1,0:T(8,128)(2,1)}, f32[32,128]{1,0:T(8,128)}, bf16[128,256]{1,0:T(8,128)(2,1)}, bf1...) custom-call(s32[1,17]{1,0:T(1,128)} %lens.1, ...), custom_call_target="tpu_custom_call" | custom-call | tf_op jit(solution)/shard_map/mixer_and_attention/pallas_call | solution.py:743
  92.0 2.8 %hand_over.1 = (bf16[128,2048]{1,0:T(8,128)(2,1)}, bf16[128,2048]{1,0:T(8,128)(2,1)}, f32[32,128]{1,0:T(8,128)}, bf16[128,256]{1,0:T(8,128)(2,1)}, bf16[128,256]...) custom-call(bf16[128,2048]{1,0:T(8,128)(2,1)} %get-tuple-element.33., ...), custom_call_target="tpu_custom_call" | custom-call | tf_op jit(solution)/shard_map/hand_over/pallas_call | solution.py:770

commit v3 on v2

--- a/solution.py
+++ b/solution.py
@@ -74,12 +74,12 @@
 def kernel(
     lens, x_in, gate_in, raw_in, b_in, c_in, rate_log, bias, skip, gain,
     dout_in, q_in, k_in, v_in, do_in,
-    gx, ggate, graw, gb, gc, grate, gskip, ggain, gq, gk, gv,
+    gx_out, ggate_out, graw, gb, gc, grate, gskip, ggain, gq_out, gk, gv,
     ls, w, mixed, carried, dy, dxin, sve, tse, rows, marks, heads,
     gram, dgram, loc, dsl, fsend, frecv, bsend, brecv, kw, vw, kall, vall,
     dacc, dsend, drecv, tsum, tmsg, tbuf, cols, dc, db, hsum, zmsg, zbuf, xmsg, xbuf,
     zlate, zlbuf, xlate, xlbuf, x, gate, raw, b, c, dout, q, k, v, do,
-    fss, frs, bss, brs, kss, krs, dss, drs, tss, trs, zss, zrs, xss, xrs, ins,
+    gx, ggate, gq, fss, frs, bss, brs, kss, krs, dss, drs, tss, trs, zss, zrs, xss, xrs, ins, outs,
 ):
     i = lax.axis_index("ctx")
     core = lax.axis_index("dp")
@@ -370,6 +370,11 @@
                 window = slice(slot * TOKENS, (slot + 1) * TOKENS)
                 kall[kv, window] = kw[slot, :, head] if slot < REACH else k[:, head]
                 vall[kv, window] = vw[slot, :, head] if slot < REACH else v[:, head]
+
+    stores = [
+        pltpu.make_async_copy(result, output, outs.at[n])
+        for n, (result, output) in enumerate(((ggate, ggate_out), (gq, gq_out), (gx, gx_out)))
+    ]
 
     f_leg_a(1)
     inside_pair(0, 0, 8)
@@ -543,6 +548,7 @@
         zmsg[pieces : pieces + 8] = nt(ones, padded(hsum[1]), HIGH)
         z_start(0)
 
+    stores[0].start()
     kv_wait(2)
     kv_start(3)
     inside_back(0, 0, pairs)
@@ -558,6 +564,7 @@
     b_leg_b(0)
     d_hop(0, 1)
     attention(1, 2, 4)
+    stores[1].start()
     b_leg_b(1)
     d_hop(1, 0)
     inside_back(1, 0, pairs)
@@ -568,6 +575,7 @@
     for stage in range(4):
         at_stage(side_sums, stage)
     early_sums()
+    heads[5] = nn(hsum[0], not_before.astype(F32), HIGH) + heads[4]
     d_hop(1, 1)
     d_hop(0, 3)
     b_leg_b(3)
@@ -580,22 +588,20 @@
     over = jnp.sum(hsum[3], axis=1, keepdims=True)
     cum_end = heads[1][:, TOKENS - 1 :]
     whole = jnp.where(begin_last < 0, jnp.exp(cum_end), 0.0)
-    log_grad = (
-        nn(hsum[0], not_before.astype(F32), HIGH)
-        + nn(tail * step * tail_sum, before.astype(F32), HIGH)
-        + heads[4]
-        + whole * over
-    )
-    rate_part = -log_grad * rate * step
+    decay = -rate * step
+    spilled = tail * step * tail_sum
+    rate_part = decay * (heads[5] + whole * over) + spilled * (cum_end - heads[1])
     zlate[...] = nt(ones, padded(rate_part), HIGH)
     z_start(1)
     d_hop(1, 2)
     for stage in range(4):
         at_stage(finish, stage)
+    stores[2].start()
     d_hop(0, 4)
     x_start(0)
     d_hop(1, 3)
 
+    log_grad = heads[5] + whole * over + nn(spilled, before.astype(F32), HIGH)
     step_grad = heads[3] / step + tail * tail_sum - rate * log_grad
     shifted = raw[...] + column(bias[...])
     graw[...] = jax.nn.sigmoid(shifted) * step_grad
@@ -614,6 +620,8 @@
     total = x_total(1)
     grate[...] = total[0:1, :n_heads]
 
+    for store in stores:
+        store.wait()
     for hop in range(REACH):
         for copy in kv_copies(hop):
             copy.wait_send()
@@ -637,15 +645,21 @@
 
 
 def hand_over(*refs):
-    results, outputs, sems = refs[:11], refs[11:22], refs[22]
+    results, outputs, held, arrived, left = refs[:11], refs[11:22], refs[22:33], refs[33], refs[34]
     copies = [
-        pltpu.make_async_copy(result, output, sems.at[n])
-        for n, (result, output) in enumerate(zip(results, outputs))
+        (
+            pltpu.make_async_copy(result, slot, arrived.at[n]),
+            pltpu.make_async_copy(slot, output, left.at[n]),
+        )
+        for n, (result, slot, output) in enumerate(zip(results, held, outputs))
     ]
-    for copy in copies:
-        copy.start()
-    for copy in copies:
-        copy.wait()
+    for first, _ in copies:
+        first.start()
+    for first, second in copies:
+        first.wait()
+        second.start()
+    for _, second in copies:
+        second.wait()
 
 
 def per_device(
@@ -679,7 +693,7 @@
         pltpu.VMEM((TOKENS, channels), F32),
         pltpu.VMEM((8, channels), F32),
         pltpu.VMEM((n_heads, channels), BF16),
-        pltpu.VMEM((5, n_heads, TOKENS), F32),
+        pltpu.VMEM((6, n_heads, TOKENS), F32),
         pltpu.VMEM((groups,) + square, F32),
         pltpu.VMEM((groups,) + square, F32),
         pltpu.VMEM(chunked, F32),
@@ -720,6 +734,9 @@
         pltpu.VMEM(narrow.shape, BF16),
         pltpu.VMEM(narrow.shape, BF16),
         pltpu.VMEM(wide.shape, BF16),
+        pltpu.VMEM(wide.shape, BF16),
+        pltpu.VMEM(wide.shape, BF16),
+        pltpu.VMEM(wide.shape, BF16),
         dma((2, chunks, TOKENS // CUT)),
         dma((2, chunks, TOKENS // CUT)),
         dma((2, chunks, TOKENS // CUT)),
@@ -735,6 +752,7 @@
         dma((2, X_SIZE * CORES)),
         dma((2, X_SIZE * CORES)),
         dma((10,)),
+        dma((3,)),
     ]
     shapes = (
         wide, wide, jax.ShapeDtypeStruct((n_heads, TOKENS), F32), narrow, narrow, head_row,
@@ -744,7 +762,7 @@
         kernel,
         out_shape=shapes,
         in_specs=[smem] + [hbm] * 5 + [vmem] * 4 + [hbm] * 5,
-        out_specs=(vmem,) * 11,
+        out_specs=(hbm, hbm) + (vmem,) * 6 + (hbm, vmem, vmem),
         scratch_shapes=scratch,
         compiler_params=pltpu.CompilerParams(
             collective_id=0, has_side_effects=True, vmem_limit_bytes=VMEM_LIMIT
@@ -770,9 +788,9 @@
     results = pl.pallas_call(
         hand_over,
         out_shape=shapes,
-        in_specs=[vmem] * 11,
+        in_specs=[anywhere] * 11,
         out_specs=(anywhere,) * 11,
-        scratch_shapes=[dma((11,))],
+        scratch_shapes=[pltpu.VMEM(a.shape, a.dtype) for a in shapes] + [dma((11,)), dma((11,))],
         compiler_params=pltpu.CompilerParams(vmem_limit_bytes=VMEM_LIMIT),
         name="hand_over",
     )(*results)

time: 95 us -> 93.6 us (0.985)
  Pallas kernels: 94.1 us -> 92.8 us
    pallas_call x1, Pallas kernels: 91.3 us -> 90.3 us  [per_device(): pl.pallas_call(kernel, out_shape=shapes, in_specs=[smem] + [hbm] * 5 + [v...]
where the time goes in v3:
time: 93.6 us; the launch traced here: 93.4 us
  Pallas kernels  92.8 us (99%)
    pallas_call x1, Pallas kernels, per_device(): pl.pallas_call(kernel, out_shape=shapes, in_specs=[smem] + [hbm] * 5 + [v...  90.3 us
    pallas_call x1, Pallas kernels, per_device(): pl.pallas_call(hand_over, out_shape=shapes, in_specs=[anywhere] * 11, out...  2.47 us

profile of v3, /device:TPU:1, one launch (start us, length us, event | category | flops | bytes accessed | tf_op | source)
XLA Modules:
  0.0 93.4 jit_solution(11177316953723668990)
XLA Ops:
  0.6 90.3 %mixer_and_attention.1 = (bf16[128,2048]{1,0:T(8,128)(2,1)}, bf16[128,2048]{1,0:T(8,128)(2,1)}, f32[32,128]{1,0:T(8,128)}, bf16[128,256]{1,0:T(8,128)(2,1)}, bf1...) custom-call(s32[1,17]{1,0:T(1,128)} %lens.1, ...), custom_call_target="tpu_custom_call" | custom-call | tf_op jit(solution)/shard_map/mixer_and_attention/pallas_call | solution.py:761
  90.9 2.5 %hand_over.1 = (bf16[128,2048]{1,0:T(8,128)(2,1)}, bf16[128,2048]{1,0:T(8,128)(2,1)}, f32[32,128]{1,0:T(8,128)}, bf16[128,256]{1,0:T(8,128)(2,1)}, bf16[128,256]...) custom-call(bf16[128,2048]{1,0:T(8,128)(2,1)} %get-tuple-element.33., ...), custom_call_target="tpu_custom_call" | custom-call | tf_op jit(solution)/shard_map/hand_over/pallas_call | solution.py:788

commit v4 on v3

--- a/solution.py
+++ b/solution.py
@@ -417,14 +417,20 @@
 
     def cotangents(ch, g):
         part = lanes(ch * CHUNK, CHUNK)
+        _, _, activation, _, scaled = gating(part)
+        gated = mixed[:, part] * activation
+        gated_grad = twice(cols[0]) * scaled - gated * twice(cols[1])
+        mixed_grad = gated_grad * activation
+        dy[:, part] = mixed_grad.astype(BF16)
+        dsl[ch] = tn(group(c, g), (mixed_grad * sve[:, part]).astype(BF16))
+
+    def gate_grads(ch, g):
+        part = lanes(ch * CHUNK, CHUNK)
         g_here, sigma, activation, out_grad, scaled = gating(part)
         here = mixed[:, part]
         gated = here * activation
         factor_col = twice(cols[0])
         gated_grad = factor_col * scaled - gated * twice(cols[1])
-        mixed_grad = gated_grad * activation
-        dy[:, part] = mixed_grad.astype(BF16)
-        dsl[ch] = tn(group(c, g), (mixed_grad * sve[:, part]).astype(BF16))
         gate_grad = gated_grad * here * sigma * (1.0 + g_here * (1.0 - sigma))
         ggate[:, part] = gate_grad.astype(BF16)
         rows[2:3, part] = jnp.sum(out_grad * gated * factor_col, axis=0, keepdims=True)
@@ -548,6 +554,8 @@
         zmsg[pieces : pieces + 8] = nt(ones, padded(hsum[1]), HIGH)
         z_start(0)
 
+    for stage in range(4):
+        at_stage(gate_grads, stage)
     stores[0].start()
     kv_wait(2)
     kv_start(3)
@@ -558,15 +566,15 @@
     attention(0, 0, 2)
     b_leg_a(2)
     attention(0, 2, 4)
+    d_hop(0, 0)
     b_leg_a(3)
-    d_hop(0, 0)
     attention(1, 0, 2)
     b_leg_b(0)
     d_hop(0, 1)
     attention(1, 2, 4)
     stores[1].start()
+    d_hop(1, 0)
     b_leg_b(1)
-    d_hop(1, 0)
     inside_back(1, 0, pairs)
     d_hop(0, 2)
     b_leg_b(2)

time: 93.6 us -> 94.3 us (level)
  no operation moved by 1% of the time
where the time goes in v4:
time: 94.3 us; the launch traced here: 94.1 us
  Pallas kernels  93.4 us (99%)
    pallas_call x1, Pallas kernels, per_device(): pl.pallas_call(kernel, out_shape=shapes, in_specs=[smem] + [hbm] * 5 + [v...  90.9 us
    pallas_call x1, Pallas kernels, per_device(): pl.pallas_call(hand_over, out_shape=shapes, in_specs=[anywhere] * 11, out...  2.47 us

profile of v4, /device:TPU:1, one launch (start us, length us, event | category | flops | bytes accessed | tf_op | source)
XLA Modules:
  0.0 94.1 jit_solution(10126652485006585556)
XLA Ops:
  0.6 90.9 %mixer_and_attention.1 = (bf16[128,2048]{1,0:T(8,128)(2,1)}, bf16[128,2048]{1,0:T(8,128)(2,1)}, f32[32,128]{1,0:T(8,128)}, bf16[128,256]{1,0:T(8,128)(2,1)}, bf1...) custom-call(s32[1,17]{1,0:T(1,128)} %lens.1, ...), custom_call_target="tpu_custom_call" | custom-call | tf_op jit(solution)/shard_map/mixer_and_attention/pallas_call | solution.py:769
  91.6 2.5 %hand_over.1 = (bf16[128,2048]{1,0:T(8,128)(2,1)}, bf16[128,2048]{1,0:T(8,128)(2,1)}, f32[32,128]{1,0:T(8,128)}, bf16[128,256]{1,0:T(8,128)(2,1)}, bf16[128,256]...) custom-call(bf16[128,2048]{1,0:T(8,128)(2,1)} %get-tuple-element.33., ...), custom_call_target="tpu_custom_call" | custom-call | tf_op jit(solution)/shard_map/hand_over/pallas_call | solution.py:796
